TPU v7x, 512 devices: a whole 4x4x16 slice. The times are simulated.
512 devices in a mesh: narrow: 16 (over x, y_lo, core), wide: 32 (over y_hi, z).
Axes of the slice: x: 4, y: 4 (y_hi: 2, y_lo: 2; y = y_hi * 2 + y_lo), z: 16, core: 2. Of those that a mesh axis runs over, the one named last changes fastest.
Arguments:
- vectors: float32 [512, 24576], P('wide', 'narrow'), may hold values from -63 to 63
- blocks: float32 [192, 5, 128, 128], P('narrow'), may hold values from -0.125 to 0.125
- columns: int32 [192, 5], P('narrow'), may hold values from 0 to 191, as said below
- lower_bound: float32 [1], replicated, may hold values from -0.8 to -0.2
- upper_bound: float32 [1], replicated, may hold values from 2.2 to 2.8
Outputs:
- basis: float32 [512, 24576], P(None, ('narrow', 'wide'))
Inputs may be any that keep to these rules, and one draw needn't show every extreme that they name: `columns`: row r holds 5 different block-rows, each within 3 of r along the closed loop of 192 block-rows (indices taken modulo 192); r - 1 and r + 1 appear in every row, r - 3 in every even row and r + 3 in every odd row.
All inputs are finite; a program needn't handle non-finite values.
Results may differ from a plain program's by a relative error of at most 0.0001.
Values sent between devices are 32-bit elements; how exact they have to be, the bound alone decides.
A program may use at most 64 MiB of HBM per device.

v0:
```python
import jax
import jax.numpy as jnp
from jax import lax
from jax.sharding import PartitionSpec as P

K = 512
REACH = 3
STEPS = 8


def extended(shard, sides, width):
    for axis, dim in sides:
        size, length = (lax.axis_size(axis), shard.shape[dim])
        up = [(i, (i + 1) % size) for i in range(size)]
        down = [(j, i) for i, j in up]
        last = lax.slice_in_dim(shard, length - width, length, axis=dim)
        first = lax.slice_in_dim(shard, 0, width, axis=dim)
        before = lax.ppermute(last, axis, up)
        after = lax.ppermute(first, axis, down)
        shard = jnp.concatenate([before, shard, after], axis=dim)
    return shard


def on_device(vectors, blocks, columns, lower_bound, upper_bound):
    vec_local = vectors.shape[0]
    row_count = vectors.shape[1]
    block_rows = blocks.shape[0]
    block_size = blocks.shape[2]
    total_blocks = block_rows * lax.axis_size("narrow")
    first_block = lax.axis_index("narrow") * block_rows
    local_index = (columns - first_block + REACH) % total_blocks
    centre = (upper_bound[0] + lower_bound[0]) * 0.5
    half_width = (upper_bound[0] - lower_bound[0]) * 0.5

    def operate(source):
        padded = extended(source, (("narrow", 1),), REACH * block_size)
        tile_rows = padded.reshape(vec_local, block_rows + 2 * REACH, block_size)
        picked = tile_rows[:, local_index, :]
        product = jnp.einsum("rsij,krsj->kri", blocks, picked, precision=lax.Precision.HIGHEST)
        return source + product.reshape(vec_local, row_count)

    previous = vectors
    current = (operate(vectors) - centre * vectors) / half_width
    for step in range(STEPS - 1):
        following = 2.0 * (operate(current) - centre * current) / half_width - previous
        previous = current
        current = following
    regrouped = lax.all_to_all(current, "wide", split_axis=1, concat_axis=0, tiled=True)
    partial_value = jnp.dot(
        regrouped, regrouped.T, preferred_element_type=jnp.float32, precision=lax.Precision.HIGHEST
    )
    gram_matrix = lax.psum(partial_value, ("narrow", "wide"))
    frob_norm = jnp.sqrt(jnp.sum(gram_matrix * gram_matrix) + 1e-06)
    rotation = 1.5 * jnp.eye(K, dtype=jnp.float32) - 0.5 * gram_matrix / frob_norm
    rotated = jnp.dot(
        rotation, regrouped, preferred_element_type=jnp.float32, precision=lax.Precision.HIGHEST
    )
    total_rows = row_count * lax.axis_size("narrow")
    return jnp.sqrt(total_rows / frob_norm) * rotated


def solution(mesh):
    return jax.shard_map(
        on_device,
        mesh=mesh,
        in_specs=(P("wide", "narrow"), P("narrow", None, None, None), P("narrow", None), P(), P()),
        out_specs=P(None, ("narrow", "wide")),
        check_vma=False,
    )
```

profile of v0, /device:TPU:1, one launch (start us, length us, event | category | flops | bytes accessed | tf_op | source)
XLA Modules:
  0.0 649.6 jit_solution(992749082751299002)
XLA Ops:
  7.4 4.6 collective-permute-start
  11.9 6.1 collective-permute-start.1
  20.3 0.9 copy_bitcast_fusion.7
  21.8 5.9 convolution_bitcast_fusion.7
  27.8 1.9 collective-permute-start.2
  29.7 5.8 collective-permute-start.3
  37.0 5.9 convolution_bitcast_fusion.6
  43.0 1.9 collective-permute-start.4
  44.9 6.4 collective-permute-start.5
  52.8 5.9 convolution_bitcast_fusion.5
  58.8 1.9 collective-permute-start.6
  60.7 6.6 %collective-permute-start.7 = (f32[16,384]{1,0:T(8,128)S(1)}, f32[16,384]{1,0:T(8,128)S(1)}, u32[]{:S(2)}, u32[]{:S(2)}) collective-permute-start(f32[16,384]{1,0:T(8,128)S(1)} %get-tuple-element.14), channel_id=1, source_target_pairs={{32,0},{64,32},{96,64},{128,96},{160,128},{192,160},{224,192},{256... | collective-permute-start | bytes 73736 | tf_op jit(solution)/shard_map/ppermute | solution.py:19
  68.6 5.9 convolution_bitcast_fusion.4
  74.7 1.9 collective-permute-start.8
  76.6 6.4 collective-permute-start.9
  84.5 5.9 convolution_bitcast_fusion.3
  90.5 1.9 collective-permute-start.10
  92.4 6.4 collective-permute-start.11
  100.3 5.9 convolution_bitcast_fusion.2
  106.3 1.9 collective-permute-start.12
  108.3 6.6 %collective-permute-start.13 = (f32[16,384]{1,0:T(8,128)S(1)}, f32[16,384]{1,0:T(8,128)S(1)}, u32[]{:S(2)}, u32[]{:S(2)}) collective-permute-start(f32[16,384]{1,0:T(8,128)S(1)} %get-tuple-element.8), channel_id=1, source_target_pairs={{32,0},{64,32},{96,64},{128,96},{160,128},{192,160},{224,192},{256... | collective-permute-start | bytes 73736 | tf_op jit(solution)/shard_map/ppermute | solution.py:19
  116.2 5.9 convolution_bitcast_fusion.1
  122.2 1.9 collective-permute-start.14
  124.1 6.4 collective-permute-start.15
  130.5 0.8 collective-permute-done.15
  132.0 5.9 convolution_bitcast_fusion
  138.6 27.7 %all_to_all.19 = f32[32,1,768]{2,1,0:T(1,128)S(1)} all-to-all(f32[32,1,768]{2,1,0:T(1,128)S(1)} %reshape.161), channel_id=1, replica_groups=mesh['narrow'=16,'wide'=32] {'wide'}, dimensions={0} | all-to-all | bytes 196608 | tf_op jit(solution)/shard_map/all_to_all | solution.py:48
  166.7 0.9 reduce
  167.8 2.0 fusion.49
  169.8 467.0 %all-reduce.2.cloned.1.call-done = f32[512,512]{1,0:T(8,128)} async-done(((f32[512,512]{1,0:T(8,128)}), f32[512,512]{1,0:T(8,128)}) %all-reduce.2.cloned.1.call-update) | async-done | bytes 1048592 | tf_op jit(solution)/shard_map/psum | solution.py:52
  636.7 2.1 multiply_reduce_fusion
  639.6 3.1 convolution_multiply_fusion
  (59 shorter events, 13.2 us)
Async XLA Ops:
  6.5 21.2 %copy-start = (f32[16,1536]{1,0:T(8,128)S(1)}, f32[16,1536]{1,0:T(8,128)}, u32[]{:S(2)}) copy-start(f32[16,1536]{1,0:T(8,128)} %param.5) | copy-start | bytes 294916
  6.5 630.2 %all-reduce.2.cloned.1.call-start = ((), (), s32[]{:S(2)}) async-start(), calls=%async_computation.1 | async-start | bytes 2097152 | tf_op jit(solution)/shard_map/psum | solution.py:52
  7.4 12.9 %collective-permute-start = (f32[16,384]{1,0:T(8,128)S(1)}, f32[16,384]{1,0:T(8,128)S(1)}, u32[]{:S(2)}, u32[]{:S(2)}) collective-permute-start(f32[16,384]{1,0:T(8,128)S(1)} %get-tuple-element.19), channel_id=1, source_target_pairs={{0,32},{32,64},{64,96},{96,128},{128,160},{160,192},{192,224},{224... | collective-permute-start | bytes 73736 | tf_op jit(solution)/shard_map/ppermute | solution.py:18
  11.9 8.3 %collective-permute-start.1 = (f32[16,384]{1,0:T(8,128)S(1)}, f32[16,384]{1,0:T(8,128)S(1)}, u32[]{:S(2)}, u32[]{:S(2)}) collective-permute-start(f32[16,384]{1,0:T(8,128)S(1)} %get-tuple-element.20), channel_id=1, source_target_pairs={{32,0},{64,32},{96,64},{128,96},{160,128},{192,160},{224,192},{256... | collective-permute-start | bytes 73736 | tf_op jit(solution)/shard_map/ppermute | solution.py:19
  27.8 7.7 %collective-permute-start.2 = (f32[16,384]{1,0:T(8,128)S(1)}, f32[16,384]{1,0:T(8,128)S(1)}, u32[]{:S(2)}, u32[]{:S(2)}) collective-permute-start(f32[16,384]{1,0:T(8,128)S(1)} %get-tuple-element.17), channel_id=1, source_target_pairs={{0,32},{32,64},{64,96},{96,128},{128,160},{160,192},{192,224},{224... | collective-permute-start | bytes 73736 | tf_op jit(solution)/shard_map/ppermute | solution.py:18
  29.7 6.6 %collective-permute-start.3 = (f32[16,384]{1,0:T(8,128)S(1)}, f32[16,384]{1,0:T(8,128)S(1)}, u32[]{:S(2)}, u32[]{:S(2)}) collective-permute-start(f32[16,384]{1,0:T(8,128)S(1)} %get-tuple-element.18), channel_id=1, source_target_pairs={{32,0},{64,32},{96,64},{128,96},{160,128},{192,160},{224,192},{256... | collective-permute-start | bytes 73736 | tf_op jit(solution)/shard_map/ppermute | solution.py:19
  43.0 8.4 %collective-permute-start.4 = (f32[16,384]{1,0:T(8,128)S(1)}, f32[16,384]{1,0:T(8,128)S(1)}, u32[]{:S(2)}, u32[]{:S(2)}) collective-permute-start(f32[16,384]{1,0:T(8,128)S(1)} %get-tuple-element.15), channel_id=1, source_target_pairs={{0,32},{32,64},{64,96},{96,128},{128,160},{160,192},{192,224},{224... | collective-permute-start | bytes 73736 | tf_op jit(solution)/shard_map/ppermute | solution.py:18
  44.9 7.3 %collective-permute-start.5 = (f32[16,384]{1,0:T(8,128)S(1)}, f32[16,384]{1,0:T(8,128)S(1)}, u32[]{:S(2)}, u32[]{:S(2)}) collective-permute-start(f32[16,384]{1,0:T(8,128)S(1)} %get-tuple-element.16), channel_id=1, source_target_pairs={{32,0},{64,32},{96,64},{128,96},{160,128},{192,160},{224,192},{256... | collective-permute-start | bytes 73736 | tf_op jit(solution)/shard_map/ppermute | solution.py:19
  58.8 8.5 %collective-permute-start.6 = (f32[16,384]{1,0:T(8,128)S(1)}, f32[16,384]{1,0:T(8,128)S(1)}, u32[]{:S(2)}, u32[]{:S(2)}) collective-permute-start(f32[16,384]{1,0:T(8,128)S(1)} %get-tuple-element.13), channel_id=1, source_target_pairs={{0,32},{32,64},{64,96},{96,128},{128,160},{160,192},{192,224},{224... | collective-permute-start | bytes 73736 | tf_op jit(solution)/shard_map/ppermute | solution.py:18
  60.7 7.3 %collective-permute-start.7 = (f32[16,384]{1,0:T(8,128)S(1)}, f32[16,384]{1,0:T(8,128)S(1)}, u32[]{:S(2)}, u32[]{:S(2)}) collective-permute-start(f32[16,384]{1,0:T(8,128)S(1)} %get-tuple-element.14), channel_id=1, source_target_pairs={{32,0},{64,32},{96,64},{128,96},{160,128},{192,160},{224,192},{256... | collective-permute-start | bytes 73736 | tf_op jit(solution)/shard_map/ppermute | solution.py:19
  74.7 8.4 %collective-permute-start.8 = (f32[16,384]{1,0:T(8,128)S(1)}, f32[16,384]{1,0:T(8,128)S(1)}, u32[]{:S(2)}, u32[]{:S(2)}) collective-permute-start(f32[16,384]{1,0:T(8,128)S(1)} %get-tuple-element.11), channel_id=1, source_target_pairs={{0,32},{32,64},{64,96},{96,128},{128,160},{160,192},{192,224},{224... | collective-permute-start | bytes 73736 | tf_op jit(solution)/shard_map/ppermute | solution.py:18
  76.6 7.3 %collective-permute-start.9 = (f32[16,384]{1,0:T(8,128)S(1)}, f32[16,384]{1,0:T(8,128)S(1)}, u32[]{:S(2)}, u32[]{:S(2)}) collective-permute-start(f32[16,384]{1,0:T(8,128)S(1)} %get-tuple-element.12), channel_id=1, source_target_pairs={{32,0},{64,32},{96,64},{128,96},{160,128},{192,160},{224,192},{256... | collective-permute-start | bytes 73736 | tf_op jit(solution)/shard_map/ppermute | solution.py:19
  90.5 8.4 %collective-permute-start.10 = (f32[16,384]{1,0:T(8,128)S(1)}, f32[16,384]{1,0:T(8,128)S(1)}, u32[]{:S(2)}, u32[]{:S(2)}) collective-permute-start(f32[16,384]{1,0:T(8,128)S(1)} %get-tuple-element.9), channel_id=1, source_target_pairs={{0,32},{32,64},{64,96},{96,128},{128,160},{160,192},{192,224},{224... | collective-permute-start | bytes 73736 | tf_op jit(solution)/shard_map/ppermute | solution.py:18
  92.4 7.3 %collective-permute-start.11 = (f32[16,384]{1,0:T(8,128)S(1)}, f32[16,384]{1,0:T(8,128)S(1)}, u32[]{:S(2)}, u32[]{:S(2)}) collective-permute-start(f32[16,384]{1,0:T(8,128)S(1)} %get-tuple-element.10), channel_id=1, source_target_pairs={{32,0},{64,32},{96,64},{128,96},{160,128},{192,160},{224,192},{256... | collective-permute-start | bytes 73736 | tf_op jit(solution)/shard_map/ppermute | solution.py:19
  106.3 8.6 %collective-permute-start.12 = (f32[16,384]{1,0:T(8,128)S(1)}, f32[16,384]{1,0:T(8,128)S(1)}, u32[]{:S(2)}, u32[]{:S(2)}) collective-permute-start(f32[16,384]{1,0:T(8,128)S(1)} %get-tuple-element.7), channel_id=1, source_target_pairs={{0,32},{32,64},{64,96},{96,128},{128,160},{160,192},{192,224},{224... | collective-permute-start | bytes 73736 | tf_op jit(solution)/shard_map/ppermute | solution.py:18
  108.3 7.3 %collective-permute-start.13 = (f32[16,384]{1,0:T(8,128)S(1)}, f32[16,384]{1,0:T(8,128)S(1)}, u32[]{:S(2)}, u32[]{:S(2)}) collective-permute-start(f32[16,384]{1,0:T(8,128)S(1)} %get-tuple-element.8), channel_id=1, source_target_pairs={{32,0},{64,32},{96,64},{128,96},{160,128},{192,160},{224,192},{256... | collective-permute-start | bytes 73736 | tf_op jit(solution)/shard_map/ppermute | solution.py:19
  122.2 8.4 %collective-permute-start.14 = (f32[16,384]{1,0:T(8,128)S(1)}, f32[16,384]{1,0:T(8,128)S(1)}, u32[]{:S(2)}, u32[]{:S(2)}) collective-permute-start(f32[16,384]{1,0:T(8,128)S(1)} %get-tuple-element.5), channel_id=1, source_target_pairs={{0,32},{32,64},{64,96},{96,128},{128,160},{160,192},{192,224},{224... | collective-permute-start | bytes 73736 | tf_op jit(solution)/shard_map/ppermute | solution.py:18
  124.1 7.3 %collective-permute-start.15 = (f32[16,384]{1,0:T(8,128)S(1)}, f32[16,384]{1,0:T(8,128)S(1)}, u32[]{:S(2)}, u32[]{:S(2)}) collective-permute-start(f32[16,384]{1,0:T(8,128)S(1)} %get-tuple-element.6), channel_id=1, source_target_pairs={{32,0},{64,32},{96,64},{128,96},{160,128},{192,160},{224,192},{256... | collective-permute-start | bytes 73736 | tf_op jit(solution)/shard_map/ppermute | solution.py:19
Sparse Core Ops, SparseCore 0:
  169.9 466.8 all-reduce.1
where the time goes:
time: 651 us; the launch traced here: 650 us
  waiting for transfers between devices  472 us (73%)
  starting transfers between devices  68.8 us (11%)
  matrix products  52.4 us (8%)
  blocking collectives  27.7 us (4%)
  between operations  15.9 us (2%)
  local copies, waits for them, and re-layouts  7.24 us (1%)
    psum x1, waiting for transfers between devices, on_device(): gram_matrix = lax.psum(partial_value, ('narrow', 'wide'))  467 us
    ppermute x8, starting transfers between devices, extended(): after = lax.ppermute(first, axis, down)  50.8 us
    dot_general x8, matrix products, operate(): jnp.einsum('rsij,krsj->kri', blocks, picked, precision=lax.Precision.HIGH...  47.3 us
    all_to_all x1, blocking collectives, on_device(): lax.all_to_all(current, 'wide', split_axis=1, concat_axis=0, tiled=True)  27.7 us
    ppermute x8, starting transfers between devices, extended(): before = lax.ppermute(last, axis, up)  18 us
  transfers between devices with their start and end apart: 17, of which 8 were waited for; matrix products, arithmetic and copies ran while one was open for 0% of the time, Pallas kernels for 0%

commit v1 on v0

v1 whole, which is shorter than its diff:
```python
import functools
import math

import jax
import jax.numpy as jnp
from jax import lax
from jax.experimental import pallas as pl
from jax.experimental.pallas import tpu as pltpu
from jax.sharding import PartitionSpec as P

REACH = 3
STEPS = 8
LANES = 128
SUB = 8
HALVES = 2
Z_SIZE = 16
MESH = pl.DeviceIdType.MESH
F32 = jnp.float32
BF16 = jnp.bfloat16


def split_pair(value):
    high = value.astype(BF16).astype(F32)
    return high, value - high


def upper_blocks(count):
    return [(i, j) for i in range(count) for j in range(i, count)]


def kernel_body(
    cfg,
    cols_ref,
    low_ref,
    up_ref,
    vec_ref,
    blk_ref,
    out_ref,
    ybuf,
    wbuf,
    stage,
    local_cols,
    pack,
    arrived,
    fmat,
    amat,
    bmat,
    gram,
    plane_in,
    plane_sum,
    z_in,
    z_sum,
    full,
    ghi,
    glo,
    halo_send,
    halo_recv,
    send_sem,
    a2a_recv,
    plane_recv,
    z_recv,
    bcast_recv,
    gather_recv,
):
    narrow, wide, z_size = cfg
    rows_here, slots = cols_ref.shape
    vecs = vec_ref.shape[0]
    total = rows_here * narrow
    planes = wide // z_size
    plane = narrow * planes
    n = lax.axis_index("narrow")
    w = lax.axis_index("wide")
    z = w % z_size
    y = w // z_size
    q = y * narrow + n
    right, left = lax.rem(n + 1, narrow), lax.rem(n + narrow - 1, narrow)
    share = rows_here * LANES // wide

    def plane_device(index):
        return (index % narrow, (index // narrow) * z_size + z)

    barrier = pltpu.get_barrier_semaphore()

    def greet_wide(k, carry):
        pl.semaphore_signal(barrier, inc=1, device_id=(n, (w + k) % wide), device_id_type=MESH)
        return carry

    def greet_plane(k, carry):
        pl.semaphore_signal(barrier, inc=1, device_id=plane_device((q + k) % plane), device_id_type=MESH)
        return carry

    lax.fori_loop(1, wide, greet_wide, 0)
    lax.fori_loop(1, plane, greet_plane, 0)

    first = n * rows_here
    for r in range(rows_here):
        for s in range(slots):
            at = cols_ref[r, s] - first + REACH
            at = jnp.where(at < 0, at + total, at)
            at = jnp.where(at >= total, at - total, at)
            local_cols[r, s] = jnp.minimum(at, rows_here + 2 * REACH - 1)

    for b in range(rows_here):
        ybuf[0, REACH + b] = vec_ref[:, b * LANES : (b + 1) * LANES]

    def split_blocks(r, carry):
        for s in range(slots):
            high, low = split_pair(blk_ref[r, s])
            wbuf[r, 0:LANES, s * LANES : (s + 1) * LANES] = high.astype(BF16)
            wbuf[r, LANES : 2 * LANES, s * LANES : (s + 1) * LANES] = low.astype(BF16)
        return carry

    lax.fori_loop(0, rows_here, split_blocks, 0)

    pl.semaphore_wait(barrier, wide + plane - 2)

    def halo_copies(j):
        leftward = pltpu.make_async_remote_copy(
            src_ref=ybuf.at[j, pl.ds(REACH, REACH)],
            dst_ref=ybuf.at[j, pl.ds(rows_here + REACH, REACH)],
            send_sem=halo_send.at[j, 0],
            recv_sem=halo_recv.at[j, 0],
            device_id=(left, w),
            device_id_type=MESH,
        )
        rightward = pltpu.make_async_remote_copy(
            src_ref=ybuf.at[j, pl.ds(rows_here, REACH)],
            dst_ref=ybuf.at[j, pl.ds(0, REACH)],
            send_sem=halo_send.at[j, 1],
            recv_sem=halo_recv.at[j, 1],
            device_id=(right, w),
            device_id_type=MESH,
        )
        return leftward, rightward

    for copy in halo_copies(0):
        copy.start()

    centre = jnp.full((vecs, LANES), (up_ref[0] + low_ref[0]) * 0.5, F32)
    inverse = 1.0 / jnp.full((vecs, LANES), (up_ref[0] - low_ref[0]) * 0.5, F32)
    keep = 1.0 - centre

    def put_stage(j, b):
        high, low = split_pair(ybuf[j, b])
        stage[b, 0:vecs, :] = high.astype(BF16)
        stage[b, vecs : 2 * vecs, :] = low.astype(BF16)

    edge = [r for r in range(rows_here) if r < REACH or r >= rows_here - REACH]
    inner = [r for r in range(rows_here) if r not in edge]

    def step(j, carry):
        alpha = inverse * jnp.where(j == 0, 1.0, 2.0).astype(F32)
        beta = jnp.where(j == 0, 0.0, 1.0).astype(F32)
        before = jnp.maximum(j - 1, 0)

        def row(r):
            x = jnp.concatenate([stage[local_cols[r, s]] for s in range(slots)], axis=1)
            o = lax.dot_general(x, wbuf[r], (((1,), (1,)), ((), ())), preferred_element_type=F32)
            prod = (o[:vecs, LANES:] + o[vecs:, :LANES]) + o[vecs:, LANES:] + o[:vecs, :LANES]
            ybuf[j + 1, REACH + r] = (keep * ybuf[j, REACH + r] + prod) * alpha - beta * ybuf[before, REACH + r]

        for b in range(REACH, REACH + rows_here):
            put_stage(j, b)
        for copy in halo_copies(j):
            copy.wait()
        for b in range(REACH):
            put_stage(j, b)
            put_stage(j, REACH + rows_here + b)
        for r in edge:
            row(r)

        @pl.when(j < STEPS - 1)
        def _():
            for copy in halo_copies(j + 1):
                copy.start()

        for r in inner:
            row(r)
        return carry

    lax.fori_loop(0, STEPS, step, 0)

    lane = lax.broadcasted_iota(jnp.int32, (SUB, LANES), 1)
    period = math.lcm(LANES, share) // share
    span = math.lcm(LANES, share) // LANES

    def pack_group(g, carry):
        for p in range(period):
            b0, off = divmod(p * share, LANES)
            parts = []
            for h in range(HALVES):
                here = ybuf[STEPS, REACH + g * span + b0, h * SUB : (h + 1) * SUB, :]
                part = pltpu.roll(here, (h * share - off) % LANES, 1) if (h * share - off) % LANES else here
                if off + share > LANES:
                    after = ybuf[STEPS, REACH + g * span + b0 + 1, h * SUB : (h + 1) * SUB, :]
                    part2 = pltpu.roll(after, (h * share + LANES - off) % LANES, 1)
                    part = jnp.where(lane < h * share + LANES - off, part, part2)
                parts.append(part)
            pack[g * period + p] = jnp.where(lane < share, parts[0], parts[1])
        return carry

    lax.fori_loop(0, wide // period, pack_group, 0)

    def a2a_copy(peer, slot):
        return pltpu.make_async_remote_copy(
            src_ref=pack.at[peer],
            dst_ref=arrived.at[slot],
            send_sem=send_sem.at[peer],
            recv_sem=a2a_recv.at[slot],
            device_id=(n, peer),
            device_id_type=MESH,
        )

    def a2a_start(k, carry):
        a2a_copy((w + k) % wide, w).start()
        return carry

    def a2a_wait(k, carry):
        peer = (w + k) % wide
        a2a_copy(peer, peer).wait()
        return carry

    lax.fori_loop(1, wide, a2a_start, 0)
    arrived[w] = pack[w]
    lax.fori_loop(1, wide, a2a_wait, 0)

    lane2 = lax.broadcasted_iota(jnp.int32, (HALVES * SUB, LANES), 1)

    def unpack(v, carry):
        tile = arrived[v]
        x = jnp.concatenate([tile, pltpu.roll(tile, LANES - share, 1)], axis=0)
        x = jnp.where(lane2 < share, x, 0.0)
        high, low = split_pair(x)
        rows = pl.ds(pl.multiple_of(v * HALVES * SUB, HALVES * SUB), HALVES * SUB)
        fmat[rows, :] = x
        amat[rows, 0:LANES] = (high + pltpu.roll(low, share, 1)).astype(BF16)
        amat[rows, LANES : 2 * LANES] = high.astype(BF16)
        bmat[rows, 0:LANES] = (high + pltpu.roll(high, share, 1)).astype(BF16)
        bmat[rows, LANES : 2 * LANES] = low.astype(BF16)
        return carry

    lax.fori_loop(0, wide, unpack, 0)

    side = fmat.shape[0] // LANES
    blocks_of = upper_blocks(side)
    for index, (i, j) in enumerate(blocks_of):
        gram[index * LANES : (index + 1) * LANES, :] = lax.dot_general(
            amat[i * LANES : (i + 1) * LANES, :],
            bmat[j * LANES : (j + 1) * LANES, :],
            (((1,), (1,)), ((), ())),
            preferred_element_type=F32,
        )

    chunk = gram.shape[0] // plane

    def chunk_at(index):
        return pl.ds(pl.multiple_of(index * chunk, SUB), chunk)

    def plane_copy(peer, slot):
        return pltpu.make_async_remote_copy(
            src_ref=gram.at[chunk_at(peer)],
            dst_ref=plane_in.at[slot],
            send_sem=send_sem.at[peer],
            recv_sem=plane_recv.at[slot],
            device_id=plane_device(peer),
            device_id_type=MESH,
        )

    def plane_start(k, carry):
        plane_copy((q + k) % plane, q).start()
        return carry

    def plane_wait(k, acc):
        peer = (q + k) % plane
        plane_copy(peer, peer).wait()
        return acc + plane_in[peer]

    lax.fori_loop(1, plane, plane_start, 0)
    plane_sum[...] = lax.fori_loop(1, plane, plane_wait, gram[chunk_at(q), :])

    tiles = chunk // SUB
    stride = z_size // tiles
    away = (z - n + z_size * narrow) % z_size
    owner = (away % stride == 0) & (away < stride * tiles)
    mine = jnp.minimum(away // stride, tiles - 1)

    def owner_z(t):
        return (t * stride + n) % z_size

    def z_copy(t, slot):
        return pltpu.make_async_remote_copy(
            src_ref=plane_sum.at[pl.ds(t * SUB, SUB)],
            dst_ref=z_in.at[slot],
            send_sem=send_sem.at[t],
            recv_sem=z_recv.at[slot],
            device_id=(n, y * z_size + owner_z(t)),
            device_id_type=MESH,
        )

    def tile_at(t):
        return pl.ds(pl.multiple_of(q * chunk + t * SUB, SUB), SUB)

    def bcast_copy(peer_z, t):
        return pltpu.make_async_remote_copy(
            src_ref=z_sum,
            dst_ref=full.at[tile_at(t)],
            send_sem=send_sem.at[peer_z],
            recv_sem=bcast_recv.at[t],
            device_id=(n, y * z_size + peer_z),
            device_id_type=MESH,
        )

    for t in range(tiles):

        @pl.when(owner_z(t) != z)
        def _():
            z_copy(t, z).start()

    @pl.when(owner)
    def _():
        def take(k, acc):
            peer = (z + k) % z_size
            z_copy(mine, peer).wait_recv()
            return acc + z_in[peer]

        own = plane_sum[pl.ds(pl.multiple_of(mine * SUB, SUB), SUB), :]
        z_sum[...] = lax.fori_loop(1, z_size, take, own)

    for t in range(tiles):

        @pl.when(owner_z(t) != z)
        def _():
            z_copy(t, z).wait_send()

    @pl.when(owner)
    def _():
        def give(k, carry):
            bcast_copy((z + k) % z_size, mine).start()
            return carry

        def given(k, carry):
            bcast_copy((z + k) % z_size, mine).wait_send()
            return carry

        lax.fori_loop(1, z_size, give, 0)
        full[tile_at(mine), :] = z_sum[...]
        lax.fori_loop(1, z_size, given, 0)

    for t in range(tiles):

        @pl.when(owner_z(t) != z)
        def _():
            bcast_copy(z, t).wait_recv()

    def gather_copy(peer, slot):
        return pltpu.make_async_remote_copy(
            src_ref=full.at[chunk_at(slot)],
            dst_ref=full.at[chunk_at(slot)],
            send_sem=send_sem.at[peer],
            recv_sem=gather_recv.at[slot],
            device_id=plane_device(peer),
            device_id_type=MESH,
        )

    def gather_start(k, carry):
        gather_copy((q + k) % plane, q).start()
        return carry

    def gather_wait(k, carry):
        peer = (q + k) % plane
        gather_copy(peer, peer).wait()
        return carry

    lax.fori_loop(1, plane, gather_start, 0)
    lax.fori_loop(1, plane, gather_wait, 0)

    squares = jnp.zeros((SUB, LANES), F32)
    for index, (i, j) in enumerate(blocks_of):
        block = full[index * LANES : (index + 1) * LANES, :]
        power = jnp.sum((block * block).reshape(LANES // SUB, SUB, LANES), axis=0)
        squares = squares + (power if i == j else 2.0 * power)
        high, low = split_pair(block)
        ghi[i * LANES : (i + 1) * LANES, j * LANES : (j + 1) * LANES] = high.astype(BF16)
        glo[i * LANES : (i + 1) * LANES, j * LANES : (j + 1) * LANES] = low.astype(BF16)
        if i != j:
            ghi[j * LANES : (j + 1) * LANES, i * LANES : (i + 1) * LANES] = high.T.astype(BF16)
            glo[j * LANES : (j + 1) * LANES, i * LANES : (i + 1) * LANES] = low.T.astype(BF16)

    frob = jnp.sqrt(jnp.sum(squares, keepdims=True) + 1e-06)
    scale = jnp.sqrt((total * LANES) / frob)
    main = 1.5 * scale
    cross = 0.5 * scale / frob
    fpair = amat[:, 0:LANES]
    for i in range(side):
        rows = slice(i * LANES, (i + 1) * LANES)
        zhi = jnp.dot(ghi[rows, :], fpair, preferred_element_type=F32)
        zlo = jnp.dot(glo[rows, :], fpair, preferred_element_type=F32)
        prod = (pltpu.roll(zhi, LANES - share, 1) + zlo) + zhi
        res = main * fmat[rows, :] - cross * prod
        out_ref[rows, :] = res[:, :share]


def on_device(cfg, vectors, blocks, columns, lower_bound, upper_bound):
    narrow, wide, z_size = cfg
    vecs, width = vectors.shape
    rows_here, slots = columns.shape
    count = vecs * wide
    side = count // LANES
    plane = narrow * (wide // z_size)
    gram_rows = len(upper_blocks(side)) * LANES
    chunk = gram_rows // plane
    ext = rows_here + 2 * REACH
    smem = pl.BlockSpec(memory_space=pltpu.SMEM)
    vmem = pl.BlockSpec(memory_space=pltpu.VMEM)
    dma = pltpu.SemaphoreType.DMA
    return pl.pallas_call(
        functools.partial(kernel_body, cfg),
        out_shape=jax.ShapeDtypeStruct((count, width // wide), F32),
        in_specs=[smem, smem, smem, vmem, vmem],
        out_specs=vmem,
        scratch_shapes=[
            pltpu.VMEM((STEPS + 1, ext, vecs, LANES), F32),
            pltpu.VMEM((rows_here, 2 * LANES, slots * LANES), BF16),
            pltpu.VMEM((ext, 2 * vecs, LANES), BF16),
            pltpu.SMEM((rows_here, slots), jnp.int32),
            pltpu.VMEM((wide, SUB, LANES), F32),
            pltpu.VMEM((wide, SUB, LANES), F32),
            pltpu.VMEM((count, LANES), F32),
            pltpu.VMEM((count, 2 * LANES), BF16),
            pltpu.VMEM((count, 2 * LANES), BF16),
            pltpu.VMEM((gram_rows, LANES), F32),
            pltpu.VMEM((plane, chunk, LANES), F32),
            pltpu.VMEM((chunk, LANES), F32),
            pltpu.VMEM((z_size, SUB, LANES), F32),
            pltpu.VMEM((SUB, LANES), F32),
            pltpu.VMEM((gram_rows, LANES), F32),
            pltpu.VMEM((count, count), BF16),
            pltpu.VMEM((count, count), BF16),
            dma((STEPS, 2)),
            dma((STEPS, 2)),
            dma((max(wide, plane, z_size),)),
            dma((wide,)),
            dma((plane,)),
            dma((z_size,)),
            dma((chunk // SUB,)),
            dma((plane,)),
        ],
        compiler_params=pltpu.CompilerParams(
            collective_id=0, has_side_effects=True, vmem_limit_bytes=48 * 1024 * 1024
        ),
    )(columns, lower_bound, upper_bound, vectors, blocks)


def solution(mesh):
    cfg = (mesh.shape["narrow"], mesh.shape["wide"], Z_SIZE)
    return jax.shard_map(
        functools.partial(on_device, cfg),
        mesh=mesh,
        in_specs=(P("wide", "narrow"), P("narrow", None, None, None), P("narrow", None), P(), P()),
        out_specs=P(None, ("narrow", "wide")),
        check_vma=False,
    )
```

time: 651 us -> 105 us (0.16)
  waiting for transfers between devices: 472 us -> 0 us
  Pallas kernels: 0 us -> 99.3 us
  starting transfers between devices: 68.8 us -> 0 us
  matrix products: 52.4 us -> 0 us
  blocking collectives: 27.7 us -> 0 us
  between operations: 15.9 us -> 1.31 us
    psum x1 -> x0, waiting for transfers between devices: 467 us -> none  [on_device(): gram_matrix = lax.psum(partial_value, ('narrow', 'wide'))]
    pallas_call x0 -> x1, Pallas kernels: none -> 99.3 us  [on_device(): pl.pallas_call(functools.partial(kernel_body, cfg), out_shape=jax.ShapeDt...]
    ppermute x16 -> x0, starting transfers between devices: 68.8 us -> none  [the longest x8 50.8 us: extended(): after = lax.ppermute(first, axis, down)]
    dot_general x10 -> x0, matrix products: 52.4 us -> none  [the longest x8 47.3 us: operate(): jnp.einsum('rsij,krsj->kri', blocks, picked, precision=lax.Precision.HIGH...]
    all_to_all x1 -> x0, blocking collectives: 27.7 us -> none  [on_device(): lax.all_to_all(current, 'wide', split_axis=1, concat_axis=0, tiled=True)]
  transfers between devices with their start and end apart: 17 -> 0, of which waited for: 8 -> 0; matrix products, arithmetic and copies ran while one was open for 0% -> 0% of each run, Pallas kernels for 0% -> 0%
where the time goes in v1:
time: 105 us
  Pallas kernels  99.3 us (95%)
  local copies, waits for them, and re-layouts  4.53 us (4%)
  between operations  1.31 us (1%)
    pallas_call x1, Pallas kernels, on_device(): pl.pallas_call(functools.partial(kernel_body, cfg), out_shape=jax.ShapeDt...  99.3 us
    unnamed x5, local copies, waits for them, and re-layouts  3.78 us

profile of v1, /device:TPU:1, one launch (start us, length us, event | category | flops | bytes accessed | tf_op | source)
XLA Modules:
  0.0 105.1 jit_solution(8575223920782394250)
XLA Ops:
  1.3 0.8 copy.6.cols_ref
  2.1 0.0 copy-start
  2.1 2.1 %copy-done = f32[12,5,128,128]{3,2,1,0:T(8,128)S(1)} copy-done((f32[12,5,128,128]{3,2,1,0:T(8,128)S(1)}, f32[12,5,128,128]{3,2,1,0:T(8,128)}, u32[]{:S(2)}) %copy-start) | copy-done | bytes 3932184
  4.2 0.0 copy-start.1
  4.2 0.9 copy-done.1
  5.1 99.3 %shard_map.55 = f32[512,48]{1,0:T(8,128)S(1)} custom-call(s32[12,5]{1,0:T(8,128)S(1)} %copy.6.cols_ref, f32[1]{0:T(128)S(6)} %copy.8.low_ref, f32[1]{0:T(128)S(6)} %copy.9.up_ref, f32[16,1536]{1,0:T(8,128)S(1)} %copy-done.1, f32[12,5,128,128]{3,2,1,0:T(8,128)S(1)} %copy-done), custom_call_target="tpu_custom_call" | custom-call | tf_op jit(solution)/shard_map/pallas_call | solution.py:416
  104.4 0.8 copy.7
Async XLA Ops:
  2.1 2.1 %copy-start = (f32[12,5,128,128]{3,2,1,0:T(8,128)S(1)}, f32[12,5,128,128]{3,2,1,0:T(8,128)}, u32[]{:S(2)}) copy-start(f32[12,5,128,128]{3,2,1,0:T(8,128)} %blk_ref.1) | copy-start | bytes 11796484
  4.2 0.9 copy-start.1

commit v2 on v1

--- a/solution.py
+++ b/solution.py
@@ -1,5 +1,4 @@
 import functools
-import math
 
 import jax
 import jax.numpy as jnp
@@ -40,6 +39,8 @@
     wbuf,
     stage,
     local_cols,
+    cols_in,
+    blocks_in,
     pack,
     arrived,
     fmat,
@@ -53,6 +54,9 @@
     full,
     ghi,
     glo,
+    load_sem,
+    row_sem,
+    relay,
     halo_send,
     halo_recv,
     send_sem,
@@ -63,7 +67,7 @@
     gather_recv,
 ):
     narrow, wide, z_size = cfg
-    rows_here, slots = cols_ref.shape
+    slots, rows_here = cols_ref.shape
     vecs = vec_ref.shape[0]
     total = rows_here * narrow
     planes = wide // z_size
@@ -79,127 +83,140 @@
     def plane_device(index):
         return (index % narrow, (index // narrow) * z_size + z)
 
+    def ring(dy, dz):
+        return (n, ((y + dy) % (wide // z_size)) * z_size + (z + dz) % z_size)
+
+    steps_y = {1: (), 2: (1,)}.get(wide // z_size, (1, wide // z_size - 1))
+    circle = [(left, w), (right, w), ring(0, 1), ring(0, z_size - 1)] + [ring(dy, 0) for dy in steps_y]
+
+    edges = [list(range(REACH)), list(range(rows_here - REACH, rows_here))]
+    inner = list(range(REACH, rows_here - REACH))
+
+    load_cols = pltpu.make_async_copy(cols_ref, cols_in, load_sem.at[0])
+    load_cols.start()
+    load_vec = [
+        pltpu.make_async_copy(vec_ref.at[:, pl.ds(b * LANES, LANES)], ybuf.at[0, REACH + b], load_sem.at[1])
+        for b in range(rows_here)
+    ]
+    for copy in load_vec:
+        copy.start()
+    load_rows = [pltpu.make_async_copy(blk_ref.at[r], blocks_in.at[r], row_sem.at[r]) for r in range(rows_here)]
+    for r in edges[0] + edges[1] + inner:
+        load_rows[r].start()
+
     barrier = pltpu.get_barrier_semaphore()
-
-    def greet_wide(k, carry):
-        pl.semaphore_signal(barrier, inc=1, device_id=(n, (w + k) % wide), device_id_type=MESH)
-        return carry
-
-    def greet_plane(k, carry):
-        pl.semaphore_signal(barrier, inc=1, device_id=plane_device((q + k) % plane), device_id_type=MESH)
-        return carry
-
-    lax.fori_loop(1, wide, greet_wide, 0)
-    lax.fori_loop(1, plane, greet_plane, 0)
-
+    for device in circle:
+        pl.semaphore_signal(barrier, inc=1, device_id=device, device_id_type=MESH)
+
+    load_cols.wait()
     first = n * rows_here
     for r in range(rows_here):
         for s in range(slots):
-            at = cols_ref[r, s] - first + REACH
+            at = cols_in[s, r] - first + REACH
             at = jnp.where(at < 0, at + total, at)
             at = jnp.where(at >= total, at - total, at)
             local_cols[r, s] = jnp.minimum(at, rows_here + 2 * REACH - 1)
-
-    for b in range(rows_here):
-        ybuf[0, REACH + b] = vec_ref[:, b * LANES : (b + 1) * LANES]
-
-    def split_blocks(r, carry):
-        for s in range(slots):
-            high, low = split_pair(blk_ref[r, s])
-            wbuf[r, 0:LANES, s * LANES : (s + 1) * LANES] = high.astype(BF16)
-            wbuf[r, LANES : 2 * LANES, s * LANES : (s + 1) * LANES] = low.astype(BF16)
-        return carry
-
-    lax.fori_loop(0, rows_here, split_blocks, 0)
-
-    pl.semaphore_wait(barrier, wide + plane - 2)
-
-    def halo_copies(j):
-        leftward = pltpu.make_async_remote_copy(
-            src_ref=ybuf.at[j, pl.ds(REACH, REACH)],
-            dst_ref=ybuf.at[j, pl.ds(rows_here + REACH, REACH)],
-            send_sem=halo_send.at[j, 0],
-            recv_sem=halo_recv.at[j, 0],
-            device_id=(left, w),
-            device_id_type=MESH,
-        )
-        rightward = pltpu.make_async_remote_copy(
-            src_ref=ybuf.at[j, pl.ds(rows_here, REACH)],
-            dst_ref=ybuf.at[j, pl.ds(0, REACH)],
-            send_sem=halo_send.at[j, 1],
-            recv_sem=halo_recv.at[j, 1],
-            device_id=(right, w),
-            device_id_type=MESH,
-        )
-        return leftward, rightward
-
-    for copy in halo_copies(0):
-        copy.start()
+    whole = ybuf.at[0, pl.ds(REACH, rows_here)]
+    pltpu.make_async_copy(whole, whole, load_sem.at[1]).wait()
+
+    pl.semaphore_wait(barrier, len(circle))
+
+    def pass_word(j):
+        for device in circle:
+            pl.semaphore_signal(relay.at[j], inc=1, device_id=device, device_id_type=MESH)
+
+    def halo_copy(j, side):
+        return pltpu.make_async_remote_copy(
+            src_ref=ybuf.at[j, pl.ds(rows_here if side else REACH, REACH)],
+            dst_ref=ybuf.at[j, pl.ds(0 if side else rows_here + REACH, REACH)],
+            send_sem=halo_send.at[j, side],
+            recv_sem=halo_recv.at[j, side],
+            device_id=(right if side else left, w),
+            device_id_type=MESH,
+        )
+
+    halo_copy(0, 0).start()
+    halo_copy(0, 1).start()
+    pass_word(0)
 
     centre = jnp.full((vecs, LANES), (up_ref[0] + low_ref[0]) * 0.5, F32)
     inverse = 1.0 / jnp.full((vecs, LANES), (up_ref[0] - low_ref[0]) * 0.5, F32)
     keep = 1.0 - centre
-
-    def put_stage(j, b):
-        high, low = split_pair(ybuf[j, b])
-        stage[b, 0:vecs, :] = high.astype(BF16)
-        stage[b, vecs : 2 * vecs, :] = low.astype(BF16)
-
-    edge = [r for r in range(rows_here) if r < REACH or r >= rows_here - REACH]
-    inner = [r for r in range(rows_here) if r not in edge]
-
-    def step(j, carry):
-        alpha = inverse * jnp.where(j == 0, 1.0, 2.0).astype(F32)
-        beta = jnp.where(j == 0, 0.0, 1.0).astype(F32)
-        before = jnp.maximum(j - 1, 0)
-
+    twice = 2.0 * inverse
+
+    def put_stage(j, blocks):
+        for b in blocks:
+            high, low = split_pair(ybuf[j, b])
+            stage[b, 0:vecs, :] = high.astype(BF16)
+            stage[b, vecs : 2 * vecs, :] = low.astype(BF16)
+
+    def prepare(r):
+        load_rows[r].wait()
+        for s in range(slots):
+            high, low = split_pair(blocks_in[r, s])
+            wbuf[r, 0:LANES, s * LANES : (s + 1) * LANES] = high.astype(BF16)
+            wbuf[r, LANES : 2 * LANES, s * LANES : (s + 1) * LANES] = low.astype(BF16)
+
+    def step(j, is_first):
         def row(r):
             x = jnp.concatenate([stage[local_cols[r, s]] for s in range(slots)], axis=1)
             o = lax.dot_general(x, wbuf[r], (((1,), (1,)), ((), ())), preferred_element_type=F32)
             prod = (o[:vecs, LANES:] + o[vecs:, :LANES]) + o[vecs:, LANES:] + o[:vecs, :LANES]
-            ybuf[j + 1, REACH + r] = (keep * ybuf[j, REACH + r] + prod) * alpha - beta * ybuf[before, REACH + r]
-
-        for b in range(REACH, REACH + rows_here):
-            put_stage(j, b)
-        for copy in halo_copies(j):
-            copy.wait()
-        for b in range(REACH):
-            put_stage(j, b)
-            put_stage(j, REACH + rows_here + b)
-        for r in edge:
+            moved = keep * ybuf[j, REACH + r] + prod
+            if is_first:
+                ybuf[j + 1, REACH + r] = moved * inverse
+            else:
+                ybuf[j + 1, REACH + r] = moved * twice - ybuf[j - 1, REACH + r]
+
+        put_stage(j, range(REACH, REACH + rows_here))
+        if is_first:
+            for r in edges[0] + edges[1]:
+                prepare(r)
+        for side in (0, 1):
+            halo_copy(j, 1 - side).wait_recv()
+            put_stage(j, range(REACH + rows_here, 2 * REACH + rows_here) if side else range(REACH))
+            for r in edges[side]:
+                row(r)
+
+            @pl.when(j < STEPS - 1)
+            def _():
+                halo_copy(j + 1, side).start()
+
+        for r in inner:
+            if is_first:
+                prepare(r)
             row(r)
+        pl.semaphore_wait(relay.at[j], len(circle))
 
         @pl.when(j < STEPS - 1)
         def _():
-            for copy in halo_copies(j + 1):
-                copy.start()
-
-        for r in inner:
-            row(r)
-        return carry
-
-    lax.fori_loop(0, STEPS, step, 0)
+            pass_word(j + 1)
+
+        for side in (0, 1):
+            halo_copy(j, side).wait_send()
+
+    def later_step(j, carry):
+        step(j, False)
+        return carry
+
+    step(0, True)
+    lax.fori_loop(1, STEPS, later_step, 0)
 
     lane = lax.broadcasted_iota(jnp.int32, (SUB, LANES), 1)
-    period = math.lcm(LANES, share) // share
-    span = math.lcm(LANES, share) // LANES
-
-    def pack_group(g, carry):
-        for p in range(period):
-            b0, off = divmod(p * share, LANES)
-            parts = []
-            for h in range(HALVES):
-                here = ybuf[STEPS, REACH + g * span + b0, h * SUB : (h + 1) * SUB, :]
-                part = pltpu.roll(here, (h * share - off) % LANES, 1) if (h * share - off) % LANES else here
-                if off + share > LANES:
-                    after = ybuf[STEPS, REACH + g * span + b0 + 1, h * SUB : (h + 1) * SUB, :]
-                    part2 = pltpu.roll(after, (h * share + LANES - off) % LANES, 1)
-                    part = jnp.where(lane < h * share + LANES - off, part, part2)
-                parts.append(part)
-            pack[g * period + p] = jnp.where(lane < share, parts[0], parts[1])
-        return carry
-
-    lax.fori_loop(0, wide // period, pack_group, 0)
+
+    for peer in range(wide):
+        b0, off = divmod(peer * share, LANES)
+        parts = []
+        for h in range(HALVES):
+            turn = (h * share - off) % LANES
+            here = ybuf[STEPS, REACH + b0, h * SUB : (h + 1) * SUB, :]
+            part = pltpu.roll(here, turn, 1) if turn else here
+            if off + share > LANES:
+                after = ybuf[STEPS, REACH + b0 + 1, h * SUB : (h + 1) * SUB, :]
+                part2 = pltpu.roll(after, turn, 1) if turn else after
+                part = jnp.where(lane < h * share + LANES - off, part, part2)
+            parts.append(part)
+        pack[peer] = jnp.where(lane < share, parts[0], parts[1])
 
     def a2a_copy(peer, slot):
         return pltpu.make_async_remote_copy(
@@ -226,20 +243,17 @@
 
     lane2 = lax.broadcasted_iota(jnp.int32, (HALVES * SUB, LANES), 1)
 
-    def unpack(v, carry):
+    for v in range(wide):
         tile = arrived[v]
         x = jnp.concatenate([tile, pltpu.roll(tile, LANES - share, 1)], axis=0)
         x = jnp.where(lane2 < share, x, 0.0)
         high, low = split_pair(x)
-        rows = pl.ds(pl.multiple_of(v * HALVES * SUB, HALVES * SUB), HALVES * SUB)
+        rows = slice(v * HALVES * SUB, (v + 1) * HALVES * SUB)
         fmat[rows, :] = x
         amat[rows, 0:LANES] = (high + pltpu.roll(low, share, 1)).astype(BF16)
         amat[rows, LANES : 2 * LANES] = high.astype(BF16)
         bmat[rows, 0:LANES] = (high + pltpu.roll(high, share, 1)).astype(BF16)
         bmat[rows, LANES : 2 * LANES] = low.astype(BF16)
-        return carry
-
-    lax.fori_loop(0, wide, unpack, 0)
 
     side = fmat.shape[0] // LANES
     blocks_of = upper_blocks(side)
@@ -397,7 +411,7 @@
         zlo = jnp.dot(glo[rows, :], fpair, preferred_element_type=F32)
         prod = (pltpu.roll(zhi, LANES - share, 1) + zlo) + zhi
         res = main * fmat[rows, :] - cross * prod
-        out_ref[rows, :] = res[:, :share]
+        out_ref[:, rows] = res.T[:share, :]
 
 
 def on_device(cfg, vectors, blocks, columns, lower_bound, upper_bound):
@@ -412,17 +426,20 @@
     ext = rows_here + 2 * REACH
     smem = pl.BlockSpec(memory_space=pltpu.SMEM)
     vmem = pl.BlockSpec(memory_space=pltpu.VMEM)
+    hbm = pl.BlockSpec(memory_space=pltpu.HBM)
     dma = pltpu.SemaphoreType.DMA
-    return pl.pallas_call(
+    turned = pl.pallas_call(
         functools.partial(kernel_body, cfg),
-        out_shape=jax.ShapeDtypeStruct((count, width // wide), F32),
-        in_specs=[smem, smem, smem, vmem, vmem],
+        out_shape=jax.ShapeDtypeStruct((width // wide, count), F32),
+        in_specs=[hbm, smem, smem, hbm, hbm],
         out_specs=vmem,
         scratch_shapes=[
             pltpu.VMEM((STEPS + 1, ext, vecs, LANES), F32),
             pltpu.VMEM((rows_here, 2 * LANES, slots * LANES), BF16),
             pltpu.VMEM((ext, 2 * vecs, LANES), BF16),
             pltpu.SMEM((rows_here, slots), jnp.int32),
+            pltpu.SMEM((slots, rows_here), jnp.int32),
+            pltpu.VMEM((rows_here, slots, LANES, LANES), F32),
             pltpu.VMEM((wide, SUB, LANES), F32),
             pltpu.VMEM((wide, SUB, LANES), F32),
             pltpu.VMEM((count, LANES), F32),
@@ -436,6 +453,9 @@
             pltpu.VMEM((gram_rows, LANES), F32),
             pltpu.VMEM((count, count), BF16),
             pltpu.VMEM((count, count), BF16),
+            dma((2,)),
+            dma((rows_here,)),
+            pltpu.SemaphoreType.REGULAR((STEPS,)),
             dma((STEPS, 2)),
             dma((STEPS, 2)),
             dma((max(wide, plane, z_size),)),
@@ -446,9 +466,10 @@
             dma((plane,)),
         ],
         compiler_params=pltpu.CompilerParams(
-            collective_id=0, has_side_effects=True, vmem_limit_bytes=48 * 1024 * 1024
+            collective_id=0, has_side_effects=True, vmem_limit_bytes=67_043_328
         ),
-    )(columns, lower_bound, upper_bound, vectors, blocks)
+    )(columns.T, lower_bound, upper_bound, vectors, blocks)
+    return turned.T
 
 
 def solution(mesh):

time: 105 us -> 93.4 us (0.89)
  Pallas kernels: 99.3 us -> 90.4 us
  local copies, waits for them, and re-layouts: 4.53 us -> 1.54 us
    pallas_call x1, Pallas kernels: 99.3 us -> 90.4 us  [on_device(): pl.pallas_call(functools.partial(kernel_body, cfg), out_shape=jax.ShapeDt...]
    unnamed x5 -> x1, local copies, waits for them, and re-layouts: 3.78 us -> 1.54 us
where the time goes in v2:
time: 93.4 us; the launch traced here: 93.2 us
  Pallas kernels  90.4 us (97%)
  local copies, waits for them, and re-layouts  1.54 us (2%)
  between operations  1.3 us (1%)
    pallas_call x1, Pallas kernels, on_device(): pl.pallas_call(functools.partial(kernel_body, cfg), out_shape=jax.ShapeDt...  90.4 us

profile of v2, /device:TPU:1, one launch (start us, length us, event | category | flops | bytes accessed | tf_op | source)
XLA Modules:
  0.0 93.2 jit_solution(2844048704357658254)
XLA Ops:
  1.3 90.4 %shard_map.55 = f32[48,512]{1,0:T(8,128)} custom-call(s32[5,12]{1,0:T(8,128)} %bitcast.3, f32[1]{0:T(128)S(6)} %copy.7.low_ref, f32[1]{0:T(128)S(6)} %copy.8.up_ref, f32[16,1536]{1,0:T(8,128)} %vec_ref.1, f32[12,5,128,128]{3,2,1,0:T(8,128)} %blk_ref.1), custom_call_target="tpu_custom_call" | custom-call | tf_op jit(solution)/shard_map/pallas_call | solution.py:431
  91.7 1.5 %copy.9 = f32[512,48]{0,1:T(8,128)} copy(f32[512,48]{0,1:T(8,128)} %bitcast.2) | data formatting | bytes 196608

commit v3 on v2

--- a/solution.py
+++ b/solution.py
@@ -61,9 +61,13 @@
     halo_recv,
     send_sem,
     a2a_recv,
+    plane_sent,
     plane_recv,
+    z_sent,
     z_recv,
+    bcast_sent,
     bcast_recv,
+    gather_sent,
     gather_recv,
 ):
     narrow, wide, z_size = cfg
@@ -228,8 +232,17 @@
             device_id_type=MESH,
         )
 
-    def a2a_start(k, carry):
-        a2a_copy((w + k) % wide, w).start()
+    half = z_size // 2
+
+    def far_first(i):
+        away = half - (i + 1) // 2
+        return jnp.where(i % 2 == 0, z_size - away, away)
+
+    planes = wide // z_size
+
+    def a2a_start(i, carry):
+        peer = ((y + planes - 1 - i % planes) % planes) * z_size + (z + far_first(i // planes)) % z_size
+        a2a_copy(peer, w).start()
         return carry
 
     def a2a_wait(k, carry):
@@ -237,7 +250,7 @@
         a2a_copy(peer, peer).wait()
         return carry
 
-    lax.fori_loop(1, wide, a2a_start, 0)
+    lax.fori_loop(0, wide - 1, a2a_start, 0)
     arrived[w] = pack[w]
     lax.fori_loop(1, wide, a2a_wait, 0)
 
@@ -266,127 +279,121 @@
         )
 
     chunk = gram.shape[0] // plane
-
-    def chunk_at(index):
-        return pl.ds(pl.multiple_of(index * chunk, SUB), chunk)
-
-    def plane_copy(peer, slot):
+    tiles = chunk // SUB
+    stride = z_size // tiles
+
+    def tile_rows(owner, t):
+        return pl.ds(pl.multiple_of(owner * chunk + t * SUB, SUB), SUB)
+
+    def owner_of(i):
+        other = (z + far_first(i)) % z_size
+        return other, (other % stride == 0) & (other < stride * tiles), jnp.minimum(other // stride, tiles - 1)
+
+    def all_bytes(ref, sem):
+        pltpu.make_async_copy(ref, ref, sem).wait()
+
+    def plane_send(i, carry):
+        _, owned, t = owner_of(i)
+
+        @pl.when(owned)
+        def _():
+            def send(k, inner_carry):
+                peer = (q + k) % plane
+                pltpu.make_async_remote_copy(
+                    src_ref=gram.at[tile_rows(peer, t)],
+                    dst_ref=plane_in.at[t, k - 1],
+                    send_sem=plane_sent.at[t],
+                    recv_sem=plane_recv.at[t],
+                    device_id=plane_device(peer),
+                    device_id_type=MESH,
+                ).start()
+                return inner_carry
+
+            lax.fori_loop(1, plane, send, 0)
+
+        return carry
+
+    lax.fori_loop(0, z_size, plane_send, 0)
+
+    def z_copy(other, t):
         return pltpu.make_async_remote_copy(
-            src_ref=gram.at[chunk_at(peer)],
-            dst_ref=plane_in.at[slot],
-            send_sem=send_sem.at[peer],
-            recv_sem=plane_recv.at[slot],
-            device_id=plane_device(peer),
+            src_ref=plane_sum.at[t],
+            dst_ref=z_in.at[(other - z + z_size) % z_size - 1],
+            send_sem=z_sent.at[t],
+            recv_sem=z_recv,
+            device_id=(n, y * z_size + other),
             device_id_type=MESH,
         )
 
-    def plane_start(k, carry):
-        plane_copy((q + k) % plane, q).start()
-        return carry
-
-    def plane_wait(k, acc):
-        peer = (q + k) % plane
-        plane_copy(peer, peer).wait()
-        return acc + plane_in[peer]
-
-    lax.fori_loop(1, plane, plane_start, 0)
-    plane_sum[...] = lax.fori_loop(1, plane, plane_wait, gram[chunk_at(q), :])
-
-    tiles = chunk // SUB
-    stride = z_size // tiles
-    away = (z - n + z_size * narrow) % z_size
-    owner = (away % stride == 0) & (away < stride * tiles)
-    mine = jnp.minimum(away // stride, tiles - 1)
-
-    def owner_z(t):
-        return (t * stride + n) % z_size
-
-    def z_copy(t, slot):
+    def bcast_copy(other, t):
         return pltpu.make_async_remote_copy(
-            src_ref=plane_sum.at[pl.ds(t * SUB, SUB)],
-            dst_ref=z_in.at[slot],
-            send_sem=send_sem.at[t],
-            recv_sem=z_recv.at[slot],
-            device_id=(n, y * z_size + owner_z(t)),
+            src_ref=z_sum,
+            dst_ref=full.at[tile_rows(q, t)],
+            send_sem=bcast_sent,
+            recv_sem=bcast_recv.at[t],
+            device_id=(n, y * z_size + other),
             device_id_type=MESH,
         )
 
-    def tile_at(t):
-        return pl.ds(pl.multiple_of(q * chunk + t * SUB, SUB), SUB)
-
-    def bcast_copy(peer_z, t):
-        return pltpu.make_async_remote_copy(
-            src_ref=z_sum,
-            dst_ref=full.at[tile_at(t)],
-            send_sem=send_sem.at[peer_z],
-            recv_sem=bcast_recv.at[t],
-            device_id=(n, y * z_size + peer_z),
-            device_id_type=MESH,
-        )
+    def plane_reduce(i, carry):
+        other, owned, t = owner_of(i)
+
+        @pl.when(owned)
+        def _():
+            all_bytes(plane_in.at[t], plane_recv.at[t])
+            plane_sum[t] = gram[tile_rows(q, t), :] + jnp.sum(plane_in[t], axis=0)
+
+        @pl.when(owned & (other != z))
+        def _():
+            z_copy(other, t).start()
+
+        return carry
+
+    lax.fori_loop(0, z_size, plane_reduce, 0)
+
+    _, owner_here, mine = owner_of(z_size - 1)
+
+    @pl.when(owner_here)
+    def _():
+        all_bytes(z_in, z_recv)
+        z_sum[...] = plane_sum[mine] + jnp.sum(z_in[...], axis=0)
+
+        def give(i, carry):
+            bcast_copy((z + far_first(i)) % z_size, mine).start()
+            return carry
+
+        lax.fori_loop(0, z_size - 1, give, 0)
+        full[tile_rows(q, mine), :] = z_sum[...]
+
+    def gather_send(i, carry):
+        other, owned, t = owner_of(z_size - 1 - i)
+
+        @pl.when(owned & (other != z))
+        def _():
+            bcast_copy(z, t).wait_recv()
+
+        @pl.when(owned)
+        def _():
+            def send(k, inner_carry):
+                peer = (q + k) % plane
+                pltpu.make_async_remote_copy(
+                    src_ref=full.at[tile_rows(q, t)],
+                    dst_ref=full.at[tile_rows(q, t)],
+                    send_sem=gather_sent.at[t],
+                    recv_sem=gather_recv.at[t],
+                    device_id=plane_device(peer),
+                    device_id_type=MESH,
+                ).start()
+                return inner_carry
+
+            lax.fori_loop(1, plane, send, 0)
+
+        return carry
+
+    lax.fori_loop(0, z_size, gather_send, 0)
 
     for t in range(tiles):
-
-        @pl.when(owner_z(t) != z)
-        def _():
-            z_copy(t, z).start()
-
-    @pl.when(owner)
-    def _():
-        def take(k, acc):
-            peer = (z + k) % z_size
-            z_copy(mine, peer).wait_recv()
-            return acc + z_in[peer]
-
-        own = plane_sum[pl.ds(pl.multiple_of(mine * SUB, SUB), SUB), :]
-        z_sum[...] = lax.fori_loop(1, z_size, take, own)
-
-    for t in range(tiles):
-
-        @pl.when(owner_z(t) != z)
-        def _():
-            z_copy(t, z).wait_send()
-
-    @pl.when(owner)
-    def _():
-        def give(k, carry):
-            bcast_copy((z + k) % z_size, mine).start()
-            return carry
-
-        def given(k, carry):
-            bcast_copy((z + k) % z_size, mine).wait_send()
-            return carry
-
-        lax.fori_loop(1, z_size, give, 0)
-        full[tile_at(mine), :] = z_sum[...]
-        lax.fori_loop(1, z_size, given, 0)
-
-    for t in range(tiles):
-
-        @pl.when(owner_z(t) != z)
-        def _():
-            bcast_copy(z, t).wait_recv()
-
-    def gather_copy(peer, slot):
-        return pltpu.make_async_remote_copy(
-            src_ref=full.at[chunk_at(slot)],
-            dst_ref=full.at[chunk_at(slot)],
-            send_sem=send_sem.at[peer],
-            recv_sem=gather_recv.at[slot],
-            device_id=plane_device(peer),
-            device_id_type=MESH,
-        )
-
-    def gather_start(k, carry):
-        gather_copy((q + k) % plane, q).start()
-        return carry
-
-    def gather_wait(k, carry):
-        peer = (q + k) % plane
-        gather_copy(peer, peer).wait()
-        return carry
-
-    lax.fori_loop(1, plane, gather_start, 0)
-    lax.fori_loop(1, plane, gather_wait, 0)
+        all_bytes(plane_in.at[t], gather_recv.at[t])
 
     squares = jnp.zeros((SUB, LANES), F32)
     for index, (i, j) in enumerate(blocks_of):
@@ -413,6 +420,25 @@
         res = main * fmat[rows, :] - cross * prod
         out_ref[:, rows] = res.T[:share, :]
 
+    for t in range(tiles):
+        all_bytes(plane_in.at[t], plane_sent.at[t])
+        all_bytes(plane_in.at[t], gather_sent.at[t])
+
+    def z_drain(i, carry):
+        other, owned, t = owner_of(i)
+
+        @pl.when(owned & (other != z))
+        def _():
+            z_copy(other, t).wait_send()
+
+        return carry
+
+    lax.fori_loop(0, z_size, z_drain, 0)
+
+    @pl.when(owner_here)
+    def _():
+        all_bytes(z_in, bcast_sent)
+
 
 def on_device(cfg, vectors, blocks, columns, lower_bound, upper_bound):
     narrow, wide, z_size = cfg
@@ -422,7 +448,7 @@
     side = count // LANES
     plane = narrow * (wide // z_size)
     gram_rows = len(upper_blocks(side)) * LANES
-    chunk = gram_rows // plane
+    tiles = gram_rows // plane // SUB
     ext = rows_here + 2 * REACH
     smem = pl.BlockSpec(memory_space=pltpu.SMEM)
     vmem = pl.BlockSpec(memory_space=pltpu.VMEM)
@@ -446,9 +472,9 @@
             pltpu.VMEM((count, 2 * LANES), BF16),
             pltpu.VMEM((count, 2 * LANES), BF16),
             pltpu.VMEM((gram_rows, LANES), F32),
-            pltpu.VMEM((plane, chunk, LANES), F32),
-            pltpu.VMEM((chunk, LANES), F32),
-            pltpu.VMEM((z_size, SUB, LANES), F32),
+            pltpu.VMEM((tiles, plane - 1, SUB, LANES), F32),
+            pltpu.VMEM((tiles, SUB, LANES), F32),
+            pltpu.VMEM((z_size - 1, SUB, LANES), F32),
             pltpu.VMEM((SUB, LANES), F32),
             pltpu.VMEM((gram_rows, LANES), F32),
             pltpu.VMEM((count, count), BF16),
@@ -458,12 +484,16 @@
             pltpu.SemaphoreType.REGULAR((STEPS,)),
             dma((STEPS, 2)),
             dma((STEPS, 2)),
-            dma((max(wide, plane, z_size),)),
             dma((wide,)),
-            dma((plane,)),
-            dma((z_size,)),
-            dma((chunk // SUB,)),
-            dma((plane,)),
+            dma((wide,)),
+            dma((tiles,)),
+            dma((tiles,)),
+            dma((tiles,)),
+            dma,
+            dma,
+            dma((tiles,)),
+            dma((tiles,)),
+            dma((tiles,)),
         ],
         compiler_params=pltpu.CompilerParams(
             collective_id=0, has_side_effects=True, vmem_limit_bytes=67_043_328

time: 93.4 us -> 86.7 us (0.928)
  Pallas kernels: 90.4 us -> 83.7 us
    pallas_call x1, Pallas kernels: 90.4 us -> 83.7 us  [on_device(): pl.pallas_call(functools.partial(kernel_body, cfg), out_shape=jax.ShapeDt...]
where the time goes in v3:
time: 86.7 us; the launch traced here: 86.6 us
  Pallas kernels  83.7 us (97%)
  local copies, waits for them, and re-layouts  1.54 us (2%)
  between operations  1.3 us (1%)
    pallas_call x1, Pallas kernels, on_device(): pl.pallas_call(functools.partial(kernel_body, cfg), out_shape=jax.ShapeDt...  83.7 us

profile of v3, /device:TPU:1, one launch (start us, length us, event | category | flops | bytes accessed | tf_op | source)
XLA Modules:
  0.0 86.6 jit_solution(10715408321113738606)
XLA Ops:
  1.3 83.7 %shard_map.55 = f32[48,512]{1,0:T(8,128)} custom-call(s32[5,12]{1,0:T(8,128)} %bitcast.3, f32[1]{0:T(128)S(6)} %copy.7.low_ref, f32[1]{0:T(128)S(6)} %copy.8.up_ref, f32[16,1536]{1,0:T(8,128)} %vec_ref.1, f32[12,5,128,128]{3,2,1,0:T(8,128)} %blk_ref.1), custom_call_target="tpu_custom_call" | custom-call | tf_op jit(solution)/shard_map/pallas_call | solution.py:457
  85.0 1.5 %copy.9 = f32[512,48]{0,1:T(8,128)} copy(f32[512,48]{0,1:T(8,128)} %bitcast.2) | data formatting | bytes 196608

commit v4 on v3

--- a/solution.py
+++ b/solution.py
@@ -84,8 +84,19 @@
     right, left = lax.rem(n + 1, narrow), lax.rem(n + narrow - 1, narrow)
     share = rows_here * LANES // wide
 
-    def plane_device(index):
-        return (index % narrow, (index // narrow) * z_size + z)
+    planes = wide // z_size
+    size_x, size_y = narrow // 4, planes * 2
+    x, full_y, core = n // 4, y * 2 + lax.rem(n // 2, 2), lax.rem(n, 2)
+
+    def hops(offset):
+        return min(offset[0], size_x - offset[0]) + min(offset[1], size_y - offset[1])
+
+    offsets = [(dx, dy, dc) for dx in range(size_x) for dy in range(size_y) for dc in range(2)][1:]
+    plane_peers = []
+    for dx, dy, dc in sorted(offsets, key=hops, reverse=True):
+        peer_y = lax.rem(full_y + dy, size_y)
+        peer_n = lax.rem(x + dx, size_x) * 4 + lax.rem(peer_y, 2) * 2 + lax.rem(core + dc, 2)
+        plane_peers.append((peer_y // 2 * narrow + peer_n, (peer_n, peer_y // 2 * z_size + z)))
 
     def ring(dy, dz):
         return (n, ((y + dy) % (wide // z_size)) * z_size + (z + dz) % z_size)
@@ -112,14 +123,6 @@
     for device in circle:
         pl.semaphore_signal(barrier, inc=1, device_id=device, device_id_type=MESH)
 
-    load_cols.wait()
-    first = n * rows_here
-    for r in range(rows_here):
-        for s in range(slots):
-            at = cols_in[s, r] - first + REACH
-            at = jnp.where(at < 0, at + total, at)
-            at = jnp.where(at >= total, at - total, at)
-            local_cols[r, s] = jnp.minimum(at, rows_here + 2 * REACH - 1)
     whole = ybuf.at[0, pl.ds(REACH, rows_here)]
     pltpu.make_async_copy(whole, whole, load_sem.at[1]).wait()
 
@@ -143,6 +146,15 @@
     halo_copy(0, 1).start()
     pass_word(0)
 
+    load_cols.wait()
+    first = n * rows_here
+    for r in range(rows_here):
+        for s in range(slots):
+            at = cols_in[s, r] - first + REACH
+            at = jnp.where(at < 0, at + total, at)
+            at = jnp.where(at >= total, at - total, at)
+            local_cols[r, s] = jnp.minimum(at, rows_here + 2 * REACH - 1)
+
     centre = jnp.full((vecs, LANES), (up_ref[0] + low_ref[0]) * 0.5, F32)
     inverse = 1.0 / jnp.full((vecs, LANES), (up_ref[0] - low_ref[0]) * 0.5, F32)
     keep = 1.0 - centre
@@ -161,54 +173,9 @@
             wbuf[r, 0:LANES, s * LANES : (s + 1) * LANES] = high.astype(BF16)
             wbuf[r, LANES : 2 * LANES, s * LANES : (s + 1) * LANES] = low.astype(BF16)
 
-    def step(j, is_first):
-        def row(r):
-            x = jnp.concatenate([stage[local_cols[r, s]] for s in range(slots)], axis=1)
-            o = lax.dot_general(x, wbuf[r], (((1,), (1,)), ((), ())), preferred_element_type=F32)
-            prod = (o[:vecs, LANES:] + o[vecs:, :LANES]) + o[vecs:, LANES:] + o[:vecs, :LANES]
-            moved = keep * ybuf[j, REACH + r] + prod
-            if is_first:
-                ybuf[j + 1, REACH + r] = moved * inverse
-            else:
-                ybuf[j + 1, REACH + r] = moved * twice - ybuf[j - 1, REACH + r]
-
-        put_stage(j, range(REACH, REACH + rows_here))
-        if is_first:
-            for r in edges[0] + edges[1]:
-                prepare(r)
-        for side in (0, 1):
-            halo_copy(j, 1 - side).wait_recv()
-            put_stage(j, range(REACH + rows_here, 2 * REACH + rows_here) if side else range(REACH))
-            for r in edges[side]:
-                row(r)
-
-            @pl.when(j < STEPS - 1)
-            def _():
-                halo_copy(j + 1, side).start()
-
-        for r in inner:
-            if is_first:
-                prepare(r)
-            row(r)
-        pl.semaphore_wait(relay.at[j], len(circle))
-
-        @pl.when(j < STEPS - 1)
-        def _():
-            pass_word(j + 1)
-
-        for side in (0, 1):
-            halo_copy(j, side).wait_send()
-
-    def later_step(j, carry):
-        step(j, False)
-        return carry
-
-    step(0, True)
-    lax.fori_loop(1, STEPS, later_step, 0)
-
     lane = lax.broadcasted_iota(jnp.int32, (SUB, LANES), 1)
 
-    for peer in range(wide):
+    def pack_one(peer):
         b0, off = divmod(peer * share, LANES)
         parts = []
         for h in range(HALVES):
@@ -232,26 +199,84 @@
             device_id_type=MESH,
         )
 
+    def send_packed(peers):
+        for peer in peers:
+            pack_one(peer)
+        for peer in peers:
+
+            @pl.when(w != peer)
+            def _():
+                a2a_copy(peer, w).start()
+
+    def last_block(peer):
+        return (peer * share + share - 1) // LANES
+
+    edge_peers = [[p for p in range(wide) if p * share // LANES < REACH], []]
+    inner_peers = [p for p in range(wide) if p * share // LANES >= REACH and last_block(p) < rows_here - REACH]
+    edge_peers[1] = [p for p in range(wide) if p not in edge_peers[0] + inner_peers]
+    assert all(last_block(p) < rows_here - REACH for p in edge_peers[0])
+
+    def step(j, is_first, is_last):
+        def row(r):
+            x = jnp.concatenate([stage[local_cols[r, s]] for s in range(slots)], axis=1)
+            o = lax.dot_general(x, wbuf[r], (((1,), (1,)), ((), ())), preferred_element_type=F32)
+            prod = (o[:vecs, LANES:] + o[vecs:, :LANES]) + o[vecs:, LANES:] + o[:vecs, :LANES]
+            moved = keep * ybuf[j, REACH + r] + prod
+            if is_first:
+                ybuf[j + 1, REACH + r] = moved * inverse
+            else:
+                ybuf[j + 1, REACH + r] = moved * twice - ybuf[j - 1, REACH + r]
+
+        put_stage(j, range(REACH, REACH + rows_here))
+        if is_first:
+            for r in edges[0] + edges[1]:
+                prepare(r)
+        if is_last:
+            for r in inner:
+                row(r)
+            pl.semaphore_wait(relay.at[j], len(circle))
+            send_packed(inner_peers)
+        for side in (0, 1):
+            halo_copy(j, 1 - side).wait_recv()
+            put_stage(j, range(REACH + rows_here, 2 * REACH + rows_here) if side else range(REACH))
+            for r in edges[side]:
+                row(r)
+            if is_last:
+                send_packed(edge_peers[side])
+            else:
+                halo_copy(j + 1, side).start()
+
+        if not is_last:
+            for r in inner:
+                if is_first:
+                    prepare(r)
+                row(r)
+            pl.semaphore_wait(relay.at[j], len(circle))
+            pass_word(j + 1)
+
+        for side in (0, 1):
+            halo_copy(j, side).wait_send()
+
+    def later_step(j, carry):
+        step(j, False, False)
+        return carry
+
+    step(0, True, False)
+    lax.fori_loop(1, STEPS - 1, later_step, 0)
+    step(STEPS - 1, False, True)
+    arrived[w] = pack[w]
+
     half = z_size // 2
 
     def far_first(i):
         away = half - (i + 1) // 2
         return jnp.where(i % 2 == 0, z_size - away, away)
-
-    planes = wide // z_size
-
-    def a2a_start(i, carry):
-        peer = ((y + planes - 1 - i % planes) % planes) * z_size + (z + far_first(i // planes)) % z_size
-        a2a_copy(peer, w).start()
-        return carry
 
     def a2a_wait(k, carry):
         peer = (w + k) % wide
         a2a_copy(peer, peer).wait()
         return carry
 
-    lax.fori_loop(0, wide - 1, a2a_start, 0)
-    arrived[w] = pack[w]
     lax.fori_loop(1, wide, a2a_wait, 0)
 
     lane2 = lax.broadcasted_iota(jnp.int32, (HALVES * SUB, LANES), 1)
@@ -297,19 +322,15 @@
 
         @pl.when(owned)
         def _():
-            def send(k, inner_carry):
-                peer = (q + k) % plane
+            for k, (peer, device) in enumerate(plane_peers):
                 pltpu.make_async_remote_copy(
                     src_ref=gram.at[tile_rows(peer, t)],
-                    dst_ref=plane_in.at[t, k - 1],
+                    dst_ref=plane_in.at[t, k],
                     send_sem=plane_sent.at[t],
                     recv_sem=plane_recv.at[t],
-                    device_id=plane_device(peer),
+                    device_id=device,
                     device_id_type=MESH,
                 ).start()
-                return inner_carry
-
-            lax.fori_loop(1, plane, send, 0)
 
         return carry
 
@@ -374,19 +395,15 @@
 
         @pl.when(owned)
         def _():
-            def send(k, inner_carry):
-                peer = (q + k) % plane
+            for _, device in plane_peers:
                 pltpu.make_async_remote_copy(
                     src_ref=full.at[tile_rows(q, t)],
                     dst_ref=full.at[tile_rows(q, t)],
                     send_sem=gather_sent.at[t],
                     recv_sem=gather_recv.at[t],
-                    device_id=plane_device(peer),
+                    device_id=device,
                     device_id_type=MESH,
                 ).start()
-                return inner_carry
-
-            lax.fori_loop(1, plane, send, 0)
 
         return carry
 

time: 86.7 us -> 85.6 us (0.987)
  Pallas kernels: 83.7 us -> 82.6 us
    pallas_call x1, Pallas kernels: 83.7 us -> 82.6 us  [on_device(): pl.pallas_call(functools.partial(kernel_body, cfg), out_shape=jax.ShapeDt...]
where the time goes in v4:
time: 85.6 us; the launch traced here: 85.4 us
  Pallas kernels  82.6 us (96%)
  local copies, waits for them, and re-layouts  1.54 us (2%)
  between operations  1.3 us (2%)
    pallas_call x1, Pallas kernels, on_device(): pl.pallas_call(functools.partial(kernel_body, cfg), out_shape=jax.ShapeDt...  82.6 us

profile of v4, /device:TPU:1, one launch (start us, length us, event | category | flops | bytes accessed | tf_op | source)
XLA Modules:
  0.0 85.4 jit_solution(4428340425132191551)
XLA Ops:
  1.3 82.6 %shard_map.55 = f32[48,512]{1,0:T(8,128)} custom-call(s32[5,12]{1,0:T(8,128)} %bitcast.3, f32[1]{0:T(128)S(6)} %copy.7.low_ref, f32[1]{0:T(128)S(6)} %copy.8.up_ref, f32[16,1536]{1,0:T(8,128)} %vec_ref.1, f32[12,5,128,128]{3,2,1,0:T(8,128)} %blk_ref.1), custom_call_target="tpu_custom_call" | custom-call | tf_op jit(solution)/shard_map/pallas_call | solution.py:474
  83.9 1.5 %copy.9 = f32[512,48]{0,1:T(8,128)} copy(f32[512,48]{0,1:T(8,128)} %bitcast.2) | data formatting | bytes 196608

commit v5 on v4

--- a/solution.py
+++ b/solution.py
@@ -38,7 +38,10 @@
     ybuf,
     wbuf,
     stage,
+    whalo,
+    partial,
     local_cols,
+    own_cols,
     cols_in,
     blocks_in,
     pack,
@@ -154,6 +157,8 @@
             at = jnp.where(at < 0, at + total, at)
             at = jnp.where(at >= total, at - total, at)
             local_cols[r, s] = jnp.minimum(at, rows_here + 2 * REACH - 1)
+            at_home = (at >= REACH) & (at < REACH + rows_here)
+            own_cols[r, s] = jnp.where(at_home, at, rows_here + 2 * REACH)
 
     centre = jnp.full((vecs, LANES), (up_ref[0] + low_ref[0]) * 0.5, F32)
     inverse = 1.0 / jnp.full((vecs, LANES), (up_ref[0] - low_ref[0]) * 0.5, F32)
@@ -165,6 +170,11 @@
             high, low = split_pair(ybuf[j, b])
             stage[b, 0:vecs, :] = high.astype(BF16)
             stage[b, vecs : 2 * vecs, :] = low.astype(BF16)
+
+    stage[rows_here + 2 * REACH] = jnp.zeros((2 * vecs, LANES), BF16)
+
+    def halo_of(side, k):
+        return range(rows_here + REACH, rows_here + REACH + k + 1) if side else range(k, REACH)
 
     def prepare(r):
         load_rows[r].wait()
@@ -172,6 +182,16 @@
             high, low = split_pair(blocks_in[r, s])
             wbuf[r, 0:LANES, s * LANES : (s + 1) * LANES] = high.astype(BF16)
             wbuf[r, LANES : 2 * LANES, s * LANES : (s + 1) * LANES] = low.astype(BF16)
+
+    def prepare_halo(side, k):
+        r = edges[side][k]
+        for i, b in enumerate(halo_of(side, k)):
+            total_block = jnp.zeros((LANES, LANES), F32)
+            for s in range(slots):
+                total_block = total_block + jnp.where(local_cols[r, s] == b, 1.0, 0.0).astype(F32) * blocks_in[r, s]
+            high, low = split_pair(total_block)
+            whalo[side, k, 0:LANES, i * LANES : (i + 1) * LANES] = high.astype(BF16)
+            whalo[side, k, LANES : 2 * LANES, i * LANES : (i + 1) * LANES] = low.astype(BF16)
 
     lane = lax.broadcasted_iota(jnp.int32, (SUB, LANES), 1)
 
@@ -217,20 +237,41 @@
     assert all(last_block(p) < rows_here - REACH for p in edge_peers[0])
 
     def step(j, is_first, is_last):
+        def gathered(o):
+            return (o[:vecs, LANES:] + o[vecs:, :LANES]) + o[vecs:, LANES:] + o[:vecs, :LANES]
+
+        def product(r):
+            x = jnp.concatenate([stage[own_cols[r, s]] for s in range(slots)], axis=1)
+            return gathered(lax.dot_general(x, wbuf[r], (((1,), (1,)), ((), ())), preferred_element_type=F32))
+
         def row(r):
-            x = jnp.concatenate([stage[local_cols[r, s]] for s in range(slots)], axis=1)
-            o = lax.dot_general(x, wbuf[r], (((1,), (1,)), ((), ())), preferred_element_type=F32)
-            prod = (o[:vecs, LANES:] + o[vecs:, :LANES]) + o[vecs:, LANES:] + o[:vecs, :LANES]
-            moved = keep * ybuf[j, REACH + r] + prod
+            moved = keep * ybuf[j, REACH + r] + product(r)
             if is_first:
                 ybuf[j + 1, REACH + r] = moved * inverse
             else:
                 ybuf[j + 1, REACH + r] = moved * twice - ybuf[j - 1, REACH + r]
 
+        def edge_own(side, k):
+            r = edges[side][k]
+            moved = keep * ybuf[j, REACH + r] + product(r)
+            partial[side, k] = moved * inverse if is_first else moved * twice - ybuf[j - 1, REACH + r]
+
+        def edge_rest(side, k):
+            places = halo_of(side, k)
+            x = jnp.concatenate([stage[b] for b in places], axis=1)
+            o = lax.dot_general(
+                x, whalo[side, k, :, : len(places) * LANES], (((1,), (1,)), ((), ())), preferred_element_type=F32
+            )
+            rest = gathered(o) * (inverse if is_first else twice)
+            ybuf[j + 1, REACH + edges[side][k]] = partial[side, k] + rest
+
         put_stage(j, range(REACH, REACH + rows_here))
-        if is_first:
-            for r in edges[0] + edges[1]:
-                prepare(r)
+        for side in (0, 1):
+            for k in range(REACH):
+                if is_first:
+                    prepare(edges[side][k])
+                    prepare_halo(side, k)
+                edge_own(side, k)
         if is_last:
             for r in inner:
                 row(r)
@@ -239,8 +280,8 @@
         for side in (0, 1):
             halo_copy(j, 1 - side).wait_recv()
             put_stage(j, range(REACH + rows_here, 2 * REACH + rows_here) if side else range(REACH))
-            for r in edges[side]:
-                row(r)
+            for k in range(REACH):
+                edge_rest(side, k)
             if is_last:
                 send_packed(edge_peers[side])
             else:
@@ -479,7 +520,10 @@
         scratch_shapes=[
             pltpu.VMEM((STEPS + 1, ext, vecs, LANES), F32),
             pltpu.VMEM((rows_here, 2 * LANES, slots * LANES), BF16),
-            pltpu.VMEM((ext, 2 * vecs, LANES), BF16),
+            pltpu.VMEM((ext + 1, 2 * vecs, LANES), BF16),
+            pltpu.VMEM((2, REACH, 2 * LANES, REACH * LANES), BF16),
+            pltpu.VMEM((2, REACH, vecs, LANES), F32),
+            pltpu.SMEM((rows_here, slots), jnp.int32),
             pltpu.SMEM((rows_here, slots), jnp.int32),
             pltpu.SMEM((slots, rows_here), jnp.int32),
             pltpu.VMEM((rows_here, slots, LANES, LANES), F32),

time: 85.6 us -> 83.8 us (0.979)
  Pallas kernels: 82.6 us -> 80.8 us
    pallas_call x1, Pallas kernels: 82.6 us -> 80.8 us  [on_device(): pl.pallas_call(functools.partial(kernel_body, cfg), out_shape=jax.ShapeDt...]
where the time goes in v5:
time: 83.8 us; the launch traced here: 83.7 us
  Pallas kernels  80.8 us (96%)
  local copies, waits for them, and re-layouts  1.54 us (2%)
  between operations  1.3 us (2%)
    pallas_call x1, Pallas kernels, on_device(): pl.pallas_call(functools.partial(kernel_body, cfg), out_shape=jax.ShapeDt...  80.8 us

profile of v5, /device:TPU:1, one launch (start us, length us, event | category | flops | bytes accessed | tf_op | source)
XLA Modules:
  0.0 83.7 jit_solution(17221946940253094422)
XLA Ops:
  1.3 80.8 %shard_map.55 = f32[48,512]{1,0:T(8,128)} custom-call(s32[5,12]{1,0:T(8,128)} %bitcast.3, f32[1]{0:T(128)S(6)} %copy.7.low_ref, f32[1]{0:T(128)S(6)} %copy.8.up_ref, f32[16,1536]{1,0:T(8,128)} %vec_ref.1, f32[12,5,128,128]{3,2,1,0:T(8,128)} %blk_ref.1), custom_call_target="tpu_custom_call" | custom-call | tf_op jit(solution)/shard_map/pallas_call | solution.py:515
  82.1 1.5 %copy.9 = f32[512,48]{0,1:T(8,128)} copy(f32[512,48]{0,1:T(8,128)} %bitcast.2) | data formatting | bytes 196608

commit v6 on v5

--- a/solution.py
+++ b/solution.py
@@ -165,11 +165,13 @@
     keep = 1.0 - centre
     twice = 2.0 * inverse
 
+    def paired(value):
+        high, low = split_pair(value)
+        return jnp.concatenate([high.astype(BF16), low.astype(BF16)], axis=0)
+
     def put_stage(j, blocks):
         for b in blocks:
-            high, low = split_pair(ybuf[j, b])
-            stage[b, 0:vecs, :] = high.astype(BF16)
-            stage[b, vecs : 2 * vecs, :] = low.astype(BF16)
+            stage[b] = paired(ybuf[j, b])
 
     stage[rows_here + 2 * REACH] = jnp.zeros((2 * vecs, LANES), BF16)
 
@@ -256,9 +258,9 @@
             moved = keep * ybuf[j, REACH + r] + product(r)
             partial[side, k] = moved * inverse if is_first else moved * twice - ybuf[j - 1, REACH + r]
 
-        def edge_rest(side, k):
+        def edge_rest(side, k, pieces):
             places = halo_of(side, k)
-            x = jnp.concatenate([stage[b] for b in places], axis=1)
+            x = jnp.concatenate([pieces[b] for b in places], axis=1)
             o = lax.dot_general(
                 x, whalo[side, k, :, : len(places) * LANES], (((1,), (1,)), ((), ())), preferred_element_type=F32
             )
@@ -279,9 +281,10 @@
             send_packed(inner_peers)
         for side in (0, 1):
             halo_copy(j, 1 - side).wait_recv()
-            put_stage(j, range(REACH + rows_here, 2 * REACH + rows_here) if side else range(REACH))
+            start = REACH + rows_here if side else 0
+            pieces = {b: paired(ybuf[j, b]) for b in range(start, start + REACH)}
             for k in range(REACH):
-                edge_rest(side, k)
+                edge_rest(side, k, pieces)
             if is_last:
                 send_packed(edge_peers[side])
             else:
@@ -306,12 +309,6 @@
     lax.fori_loop(1, STEPS - 1, later_step, 0)
     step(STEPS - 1, False, True)
     arrived[w] = pack[w]
-
-    half = z_size // 2
-
-    def far_first(i):
-        away = half - (i + 1) // 2
-        return jnp.where(i % 2 == 0, z_size - away, away)
 
     def a2a_wait(k, carry):
         peer = (w + k) % wide
@@ -346,14 +343,18 @@
 
     chunk = gram.shape[0] // plane
     tiles = chunk // SUB
-    stride = z_size // tiles
+    half = z_size // 2
+    assert tiles <= half == 8
+    near = half // 2
 
     def tile_rows(owner, t):
         return pl.ds(pl.multiple_of(owner * chunk + t * SUB, SUB), SUB)
 
     def owner_of(i):
-        other = (z + far_first(i)) % z_size
-        return other, (other % stride == 0) & (other < stride * tiles), jnp.minimum(other // stride, tiles - 1)
+        up = jnp.where(i % 2 == 0, (z_size - (i + 1) // 2) % half, (i + 1) // 2)
+        up = jnp.where(i == half - 1, near, up)
+        t = (3 * ((z + up) % half)) % half
+        return up, t < tiles, jnp.minimum(t, tiles - 1)
 
     def all_bytes(ref, sem):
         pltpu.make_async_copy(ref, ref, sem).wait()
@@ -375,64 +376,62 @@
 
         return carry
 
-    lax.fori_loop(0, z_size, plane_send, 0)
-
-    def z_copy(other, t):
+    lax.fori_loop(0, half, plane_send, 0)
+
+    def z_copy(up, t, second):
+        there = (up + second * half) % z_size
         return pltpu.make_async_remote_copy(
             src_ref=plane_sum.at[t],
-            dst_ref=z_in.at[(other - z + z_size) % z_size - 1],
-            send_sem=z_sent.at[t],
+            dst_ref=z_in.at[(there + z_size - 1) % z_size],
+            send_sem=z_sent.at[t, second],
             recv_sem=z_recv,
-            device_id=(n, y * z_size + other),
+            device_id=(n, y * z_size + (z + there) % z_size),
             device_id_type=MESH,
         )
 
-    def bcast_copy(other, t):
+    def bcast_copy(down, t):
         return pltpu.make_async_remote_copy(
             src_ref=z_sum,
             dst_ref=full.at[tile_rows(q, t)],
             send_sem=bcast_sent,
             recv_sem=bcast_recv.at[t],
-            device_id=(n, y * z_size + other),
+            device_id=(n, y * z_size + (z + z_size - down) % z_size),
             device_id_type=MESH,
         )
 
     def plane_reduce(i, carry):
-        other, owned, t = owner_of(i)
+        up, owned, t = owner_of(i)
 
         @pl.when(owned)
         def _():
             all_bytes(plane_in.at[t], plane_recv.at[t])
             plane_sum[t] = gram[tile_rows(q, t), :] + jnp.sum(plane_in[t], axis=0)
-
-        @pl.when(owned & (other != z))
-        def _():
-            z_copy(other, t).start()
+            z_copy(up, t, 1).start()
+
+        @pl.when(owned & (up != 0))
+        def _():
+            z_copy(up, t, 0).start()
 
         return carry
 
-    lax.fori_loop(0, z_size, plane_reduce, 0)
-
-    _, owner_here, mine = owner_of(z_size - 1)
+    lax.fori_loop(0, half, plane_reduce, 0)
+
+    _, owner_here, mine = owner_of(0)
 
     @pl.when(owner_here)
     def _():
         all_bytes(z_in, z_recv)
         z_sum[...] = plane_sum[mine] + jnp.sum(z_in[...], axis=0)
-
-        def give(i, carry):
-            bcast_copy((z + far_first(i)) % z_size, mine).start()
-            return carry
-
-        lax.fori_loop(0, z_size - 1, give, 0)
+        for down in [near] + [d for k in range(near - 1, 0, -1) for d in (k, -k)]:
+            bcast_copy(down, mine).start()
         full[tile_rows(q, mine), :] = z_sum[...]
 
     def gather_send(i, carry):
-        other, owned, t = owner_of(z_size - 1 - i)
-
-        @pl.when(owned & (other != z))
-        def _():
-            bcast_copy(z, t).wait_recv()
+        up, owned, t = owner_of(i)
+
+        @pl.when(owned & (up != 0))
+        def _():
+            bcast_copy(near, t).wait_recv()
 
         @pl.when(owned)
         def _():
@@ -448,7 +447,7 @@
 
         return carry
 
-    lax.fori_loop(0, z_size, gather_send, 0)
+    lax.fori_loop(0, half, gather_send, 0)
 
     for t in range(tiles):
         all_bytes(plane_in.at[t], gather_recv.at[t])
@@ -483,19 +482,23 @@
         all_bytes(plane_in.at[t], gather_sent.at[t])
 
     def z_drain(i, carry):
-        other, owned, t = owner_of(i)
-
-        @pl.when(owned & (other != z))
-        def _():
-            z_copy(other, t).wait_send()
+        up, owned, t = owner_of(i)
+
+        @pl.when(owned)
+        def _():
+            z_copy(up, t, 1).wait_send()
+
+        @pl.when(owned & (up != 0))
+        def _():
+            z_copy(up, t, 0).wait_send()
 
         return carry
 
-    lax.fori_loop(0, z_size, z_drain, 0)
+    lax.fori_loop(0, half, z_drain, 0)
 
     @pl.when(owner_here)
     def _():
-        all_bytes(z_in, bcast_sent)
+        all_bytes(z_in.at[pl.ds(0, half - 1)], bcast_sent)
 
 
 def on_device(cfg, vectors, blocks, columns, lower_bound, upper_bound):
@@ -549,7 +552,7 @@
             dma((wide,)),
             dma((tiles,)),
             dma((tiles,)),
-            dma((tiles,)),
+            dma((tiles, 2)),
             dma,
             dma,
             dma((tiles,)),

time: 83.8 us -> 83.7 us (level)
  no operation moved by 1% of the time
where the time goes in v6:
time: 83.7 us; the launch traced here: 83.6 us
  Pallas kernels  80.7 us (96%)
  local copies, waits for them, and re-layouts  1.54 us (2%)
  between operations  1.3 us (2%)
    pallas_call x1, Pallas kernels, on_device(): pl.pallas_call(functools.partial(kernel_body, cfg), out_shape=jax.ShapeDt...  80.7 us

profile of v6, /device:TPU:1, one launch (start us, length us, event | category | flops | bytes accessed | tf_op | source)
XLA Modules:
  0.0 83.6 jit_solution(6267889932712565441)
XLA Ops:
  1.3 80.7 %shard_map.55 = f32[48,512]{1,0:T(8,128)} custom-call(s32[5,12]{1,0:T(8,128)} %bitcast.3, f32[1]{0:T(128)S(6)} %copy.7.low_ref, f32[1]{0:T(128)S(6)} %copy.8.up_ref, f32[16,1536]{1,0:T(8,128)} %vec_ref.1, f32[12,5,128,128]{3,2,1,0:T(8,128)} %blk_ref.1), custom_call_target="tpu_custom_call" | custom-call | tf_op jit(solution)/shard_map/pallas_call | solution.py:518
  82.0 1.5 %copy.9 = f32[512,48]{0,1:T(8,128)} copy(f32[512,48]{0,1:T(8,128)} %bitcast.2) | data formatting | bytes 196608

commit v7 on v6

--- a/solution.py
+++ b/solution.py
@@ -135,18 +135,22 @@
         for device in circle:
             pl.semaphore_signal(relay.at[j], inc=1, device_id=device, device_id_type=MESH)
 
-    def halo_copy(j, side):
+    def halo_copy(j, side, k):
         return pltpu.make_async_remote_copy(
-            src_ref=ybuf.at[j, pl.ds(rows_here if side else REACH, REACH)],
-            dst_ref=ybuf.at[j, pl.ds(0 if side else rows_here + REACH, REACH)],
-            send_sem=halo_send.at[j, side],
-            recv_sem=halo_recv.at[j, side],
+            src_ref=ybuf.at[j, (rows_here if side else REACH) + k],
+            dst_ref=ybuf.at[j, (0 if side else rows_here + REACH) + k],
+            send_sem=halo_send.at[j, side, k],
+            recv_sem=halo_recv.at[j, side, k],
             device_id=(right if side else left, w),
             device_id_type=MESH,
         )
 
-    halo_copy(0, 0).start()
-    halo_copy(0, 1).start()
+    def deepest_first(side):
+        return range(REACH - 1, -1, -1) if side else range(REACH)
+
+    for side in (0, 1):
+        for k in range(REACH):
+            halo_copy(0, side, k).start()
     pass_word(0)
 
     load_cols.wait()
@@ -280,15 +284,16 @@
             pl.semaphore_wait(relay.at[j], len(circle))
             send_packed(inner_peers)
         for side in (0, 1):
-            halo_copy(j, 1 - side).wait_recv()
+            for k in range(REACH):
+                halo_copy(j, 1 - side, k).wait_recv()
             start = REACH + rows_here if side else 0
             pieces = {b: paired(ybuf[j, b]) for b in range(start, start + REACH)}
-            for k in range(REACH):
+            for k in deepest_first(side):
                 edge_rest(side, k, pieces)
+                if not is_last:
+                    halo_copy(j + 1, side, k).start()
             if is_last:
                 send_packed(edge_peers[side])
-            else:
-                halo_copy(j + 1, side).start()
 
         if not is_last:
             for r in inner:
@@ -299,7 +304,8 @@
             pass_word(j + 1)
 
         for side in (0, 1):
-            halo_copy(j, side).wait_send()
+            for k in range(REACH):
+                halo_copy(j, side, k).wait_send()
 
     def later_step(j, carry):
         step(j, False, False)
@@ -310,21 +316,23 @@
     step(STEPS - 1, False, True)
     arrived[w] = pack[w]
 
-    def a2a_wait(k, carry):
-        peer = (w + k) % wide
-        a2a_copy(peer, peer).wait()
-        return carry
-
-    lax.fori_loop(1, wide, a2a_wait, 0)
-
     lane2 = lax.broadcasted_iota(jnp.int32, (HALVES * SUB, LANES), 1)
 
-    for v in range(wide):
+    def wide_hops(offset):
+        return 2 * min(offset[0], planes - offset[0]) + min(offset[1], z_size - offset[1])
+
+    senders = []
+    for dy, dz in sorted([(dy, dz) for dy in range(planes) for dz in range(z_size)], key=wide_hops):
+        senders.append(lax.rem(y + dy, planes) * z_size + lax.rem(z + dz, z_size))
+    for count, v in enumerate(senders):
+        if count % 8 == 0:
+            for sender in senders[max(count, 1) : count + 8]:
+                a2a_copy(sender, sender).wait()
         tile = arrived[v]
         x = jnp.concatenate([tile, pltpu.roll(tile, LANES - share, 1)], axis=0)
         x = jnp.where(lane2 < share, x, 0.0)
         high, low = split_pair(x)
-        rows = slice(v * HALVES * SUB, (v + 1) * HALVES * SUB)
+        rows = pl.ds(pl.multiple_of(v * HALVES * SUB, HALVES * SUB), HALVES * SUB)
         fmat[rows, :] = x
         amat[rows, 0:LANES] = (high + pltpu.roll(low, share, 1)).astype(BF16)
         amat[rows, LANES : 2 * LANES] = high.astype(BF16)
@@ -546,8 +554,8 @@
             dma((2,)),
             dma((rows_here,)),
             pltpu.SemaphoreType.REGULAR((STEPS,)),
-            dma((STEPS, 2)),
-            dma((STEPS, 2)),
+            dma((STEPS, 2, REACH)),
+            dma((STEPS, 2, REACH)),
             dma((wide,)),
             dma((wide,)),
             dma((tiles,)),

time: 83.7 us -> 85.1 us (1.017)
  Pallas kernels: 80.7 us -> 82.1 us
    pallas_call x1, Pallas kernels: 80.7 us -> 82.1 us  [on_device(): pl.pallas_call(functools.partial(kernel_body, cfg), out_shape=jax.ShapeDt...]
where the time goes in v7:
time: 85.1 us; the launch traced here: 85 us
  Pallas kernels  82.1 us (96%)
  local copies, waits for them, and re-layouts  1.54 us (2%)
  between operations  1.3 us (2%)
    pallas_call x1, Pallas kernels, on_device(): pl.pallas_call(functools.partial(kernel_body, cfg), out_shape=jax.ShapeDt...  82.1 us

profile of v7, /device:TPU:1, one launch (start us, length us, event | category | flops | bytes accessed | tf_op | source)
XLA Modules:
  0.0 85.0 jit_solution(12923603316132932569)
XLA Ops:
  1.3 82.1 %shard_map.55 = f32[48,512]{1,0:T(8,128)} custom-call(s32[5,12]{1,0:T(8,128)} %bitcast.3, f32[1]{0:T(128)S(6)} %copy.7.low_ref, f32[1]{0:T(128)S(6)} %copy.8.up_ref, f32[16,1536]{1,0:T(8,128)} %vec_ref.1, f32[12,5,128,128]{3,2,1,0:T(8,128)} %blk_ref.1), custom_call_target="tpu_custom_call" | custom-call | tf_op jit(solution)/shard_map/pallas_call | solution.py:526
  83.4 1.5 %copy.9 = f32[512,48]{0,1:T(8,128)} copy(f32[512,48]{0,1:T(8,128)} %bitcast.2) | data formatting | bytes 196608

commit v8 on v6

--- a/solution.py
+++ b/solution.py
@@ -50,6 +50,8 @@
     amat,
     bmat,
     gram,
+    core_in,
+    core_sum,
     plane_in,
     plane_sum,
     z_in,
@@ -64,6 +66,10 @@
     halo_recv,
     send_sem,
     a2a_recv,
+    core_sent,
+    core_recv,
+    hand_sent,
+    hand_recv,
     plane_sent,
     plane_recv,
     z_sent,
@@ -95,11 +101,13 @@
         return min(offset[0], size_x - offset[0]) + min(offset[1], size_y - offset[1])
 
     offsets = [(dx, dy, dc) for dx in range(size_x) for dy in range(size_y) for dc in range(2)][1:]
-    plane_peers = []
+    plane_peers, core_peers = [], []
     for dx, dy, dc in sorted(offsets, key=hops, reverse=True):
         peer_y = lax.rem(full_y + dy, size_y)
         peer_n = lax.rem(x + dx, size_x) * 4 + lax.rem(peer_y, 2) * 2 + lax.rem(core + dc, 2)
         plane_peers.append((peer_y // 2 * narrow + peer_n, (peer_n, peer_y // 2 * z_size + z)))
+        if dc == 0:
+            core_peers.append(plane_peers[-1])
 
     def ring(dy, dz):
         return (n, ((y + dy) % (wide // z_size)) * z_size + (z + dz) % z_size)
@@ -331,24 +339,55 @@
         bmat[rows, 0:LANES] = (high + pltpu.roll(high, share, 1)).astype(BF16)
         bmat[rows, LANES : 2 * LANES] = low.astype(BF16)
 
+    tiles = gram.shape[2] // SUB
+    chip_here = q // 2
+
+    def place_of(tile):
+        chunk, t = divmod(tile, tiles)
+        return chunk // 2, chunk % 2, slice(t * SUB, (t + 1) * SUB)
+
     side = fmat.shape[0] // LANES
     blocks_of = upper_blocks(side)
     for index, (i, j) in enumerate(blocks_of):
-        gram[index * LANES : (index + 1) * LANES, :] = lax.dot_general(
+        block = lax.dot_general(
             amat[i * LANES : (i + 1) * LANES, :],
             bmat[j * LANES : (j + 1) * LANES, :],
             (((1,), (1,)), ((), ())),
             preferred_element_type=F32,
         )
-
-    chunk = gram.shape[0] // plane
-    tiles = chunk // SUB
+        for part in range(LANES // SUB):
+            chip, side_core, rows = place_of(index * (LANES // SUB) + part)
+            gram[chip, side_core, rows, :] = block[part * SUB : (part + 1) * SUB, :]
+
     half = z_size // 2
     assert tiles <= half == 8
     near = half // 2
 
-    def tile_rows(owner, t):
-        return pl.ds(pl.multiple_of(owner * chunk + t * SUB, SUB), SUB)
+    def rows_of(t):
+        return pl.ds(pl.multiple_of(t * SUB, SUB), SUB)
+
+    partner = (n + 1 - 2 * core, w)
+    same_core = [(peer // 2, device) for peer, device in core_peers]
+
+    def core_copy(t):
+        return pltpu.make_async_remote_copy(
+            src_ref=gram.at[:, 1 - core, rows_of(t), :],
+            dst_ref=core_in.at[t],
+            send_sem=core_sent.at[t],
+            recv_sem=core_recv.at[t],
+            device_id=partner,
+            device_id_type=MESH,
+        )
+
+    def hand_copy(t):
+        return pltpu.make_async_remote_copy(
+            src_ref=full.at[:, core, rows_of(t), :],
+            dst_ref=full.at[:, core, rows_of(t), :],
+            send_sem=hand_sent.at[t],
+            recv_sem=hand_recv.at[t],
+            device_id=partner,
+            device_id_type=MESH,
+        )
 
     def owner_of(i):
         up = jnp.where(i % 2 == 0, (z_size - (i + 1) // 2) % half, (i + 1) // 2)
@@ -359,14 +398,27 @@
     def all_bytes(ref, sem):
         pltpu.make_async_copy(ref, ref, sem).wait()
 
+    def core_send(i, carry):
+        _, owned, t = owner_of(i)
+
+        @pl.when(owned)
+        def _():
+            core_copy(t).start()
+
+        return carry
+
+    lax.fori_loop(0, half, core_send, 0)
+
     def plane_send(i, carry):
         _, owned, t = owner_of(i)
 
         @pl.when(owned)
         def _():
-            for k, (peer, device) in enumerate(plane_peers):
+            core_copy(t).wait_recv()
+            core_sum[t] = gram[:, core, rows_of(t), :] + core_in[t]
+            for k, (chip, device) in enumerate(same_core):
                 pltpu.make_async_remote_copy(
-                    src_ref=gram.at[tile_rows(peer, t)],
+                    src_ref=core_sum.at[t, chip],
                     dst_ref=plane_in.at[t, k],
                     send_sem=plane_sent.at[t],
                     recv_sem=plane_recv.at[t],
@@ -392,7 +444,7 @@
     def bcast_copy(down, t):
         return pltpu.make_async_remote_copy(
             src_ref=z_sum,
-            dst_ref=full.at[tile_rows(q, t)],
+            dst_ref=full.at[chip_here, core, rows_of(t), :],
             send_sem=bcast_sent,
             recv_sem=bcast_recv.at[t],
             device_id=(n, y * z_size + (z + z_size - down) % z_size),
@@ -405,7 +457,7 @@
         @pl.when(owned)
         def _():
             all_bytes(plane_in.at[t], plane_recv.at[t])
-            plane_sum[t] = gram[tile_rows(q, t), :] + jnp.sum(plane_in[t], axis=0)
+            plane_sum[t] = core_sum[t, chip_here] + jnp.sum(plane_in[t], axis=0)
             z_copy(up, t, 1).start()
 
         @pl.when(owned & (up != 0))
@@ -424,7 +476,7 @@
         z_sum[...] = plane_sum[mine] + jnp.sum(z_in[...], axis=0)
         for down in [near] + [d for k in range(near - 1, 0, -1) for d in (k, -k)]:
             bcast_copy(down, mine).start()
-        full[tile_rows(q, mine), :] = z_sum[...]
+        full[chip_here, core, rows_of(mine), :] = z_sum[...]
 
     def gather_send(i, carry):
         up, owned, t = owner_of(i)
@@ -435,10 +487,10 @@
 
         @pl.when(owned)
         def _():
-            for _, device in plane_peers:
+            for _, device in same_core:
                 pltpu.make_async_remote_copy(
-                    src_ref=full.at[tile_rows(q, t)],
-                    dst_ref=full.at[tile_rows(q, t)],
+                    src_ref=full.at[chip_here, core, rows_of(t), :],
+                    dst_ref=full.at[chip_here, core, rows_of(t), :],
                     send_sem=gather_sent.at[t],
                     recv_sem=gather_recv.at[t],
                     device_id=device,
@@ -449,12 +501,25 @@
 
     lax.fori_loop(0, half, gather_send, 0)
 
+    def hand_over(i, carry):
+        _, owned, t = owner_of(i)
+
+        @pl.when(owned)
+        def _():
+            all_bytes(plane_in.at[t], gather_recv.at[t])
+            hand_copy(t).start()
+
+        return carry
+
+    lax.fori_loop(0, half, hand_over, 0)
+
     for t in range(tiles):
-        all_bytes(plane_in.at[t], gather_recv.at[t])
+        all_bytes(core_in.at[t], hand_recv.at[t])
 
     squares = jnp.zeros((SUB, LANES), F32)
     for index, (i, j) in enumerate(blocks_of):
-        block = full[index * LANES : (index + 1) * LANES, :]
+        places = [place_of(index * (LANES // SUB) + part) for part in range(LANES // SUB)]
+        block = jnp.concatenate([full[chip, side_core, rows, :] for chip, side_core, rows in places], axis=0)
         power = jnp.sum((block * block).reshape(LANES // SUB, SUB, LANES), axis=0)
         squares = squares + (power if i == j else 2.0 * power)
         high, low = split_pair(block)
@@ -480,6 +545,8 @@
     for t in range(tiles):
         all_bytes(plane_in.at[t], plane_sent.at[t])
         all_bytes(plane_in.at[t], gather_sent.at[t])
+        core_copy(t).wait_send()
+        hand_copy(t).wait_send()
 
     def z_drain(i, carry):
         up, owned, t = owner_of(i)
@@ -535,12 +602,14 @@
             pltpu.VMEM((count, LANES), F32),
             pltpu.VMEM((count, 2 * LANES), BF16),
             pltpu.VMEM((count, 2 * LANES), BF16),
-            pltpu.VMEM((gram_rows, LANES), F32),
-            pltpu.VMEM((tiles, plane - 1, SUB, LANES), F32),
+            pltpu.VMEM((plane // 2, 2, tiles * SUB, LANES), F32),
+            pltpu.VMEM((tiles, plane // 2, SUB, LANES), F32),
+            pltpu.VMEM((tiles, plane // 2, SUB, LANES), F32),
+            pltpu.VMEM((tiles, plane // 2 - 1, SUB, LANES), F32),
             pltpu.VMEM((tiles, SUB, LANES), F32),
             pltpu.VMEM((z_size - 1, SUB, LANES), F32),
             pltpu.VMEM((SUB, LANES), F32),
-            pltpu.VMEM((gram_rows, LANES), F32),
+            pltpu.VMEM((plane // 2, 2, tiles * SUB, LANES), F32),
             pltpu.VMEM((count, count), BF16),
             pltpu.VMEM((count, count), BF16),
             dma((2,)),
@@ -552,6 +621,10 @@
             dma((wide,)),
             dma((tiles,)),
             dma((tiles,)),
+            dma((tiles,)),
+            dma((tiles,)),
+            dma((tiles,)),
+            dma((tiles,)),
             dma((tiles, 2)),
             dma,
             dma,

time: 83.7 us -> 83.3 us (level)
  no operation moved by 1% of the time
where the time goes in v8:
time: 83.3 us; the launch traced here: 83.2 us
  Pallas kernels  80.3 us (96%)
  local copies, waits for them, and re-layouts  1.54 us (2%)
  between operations  1.3 us (2%)
    pallas_call x1, Pallas kernels, on_device(): pl.pallas_call(functools.partial(kernel_body, cfg), out_shape=jax.ShapeDt...  80.3 us

profile of v8, /device:TPU:1, one launch (start us, length us, event | category | flops | bytes accessed | tf_op | source)
XLA Modules:
  0.0 83.2 jit_solution(12447395454648152346)
XLA Ops:
  1.3 80.3 %shard_map.55 = f32[48,512]{1,0:T(8,128)} custom-call(s32[5,12]{1,0:T(8,128)} %bitcast.3, f32[1]{0:T(128)S(6)} %copy.7.low_ref, f32[1]{0:T(128)S(6)} %copy.8.up_ref, f32[16,1536]{1,0:T(8,128)} %vec_ref.1, f32[12,5,128,128]{3,2,1,0:T(8,128)} %blk_ref.1), custom_call_target="tpu_custom_call" | custom-call | tf_op jit(solution)/shard_map/pallas_call | solution.py:585
  81.6 1.5 %copy.9 = f32[512,48]{0,1:T(8,128)} copy(f32[512,48]{0,1:T(8,128)} %bitcast.2) | data formatting | bytes 196608
